TPU v7x, 256 devices: a whole 4x4x8 slice. The times are simulated.
256 devices in a mesh: seq: 64 (over x, z, core), tp: 4 (over y).
Axes of the slice: x: 4, y: 4, z: 8, core: 2. Of those that a mesh axis runs over, the one named last changes fastest.
Arguments:
- token_ids: int32 [65536], P('seq'), may hold values from 0 to 511
- embed_table: bfloat16 [512, 2048], P(None, 'tp'), may hold values from -6 to 6
- norm_gain: float32 [2048], replicated, may hold values from 0.1 to 1.9
- in_weight: bfloat16 [2048, 3, 2048], P('seq', None, 'tp'), may hold values from -0.125 to 0.125
- short_filter: float32 [7, 3, 2048], P(None, None, 'tp'), may hold values from -2.4 to 2.4
- long_filter: bfloat16 [128, 128], P('tp'), may hold values from -0.5390625 to 0.5390625
- long_skip: float32 [2048], P('tp'), may hold values from -3 to 3
- out_weight: bfloat16 [2048, 2048], P('tp', 'seq'), may hold values from -0.125 to 0.125
Outputs:
- mixed: bfloat16 [65536, 2048], P('seq', 'tp')
All inputs are finite; a program needn't handle non-finite values.
Results may differ from a plain program's by a relative error of at most 0.012.
Values may be sent and summed in bfloat16 or wider, within the bound.
A program may use at most 64 MiB of HBM per device.

v0:
```python
import jax
import jax.numpy as jnp
from jax import lax
from jax.sharding import PartitionSpec as P


def from_behind(block, axis, distance):
    devices = range(lax.axis_size(axis))
    route = [(i - distance, i) for i in devices if i - distance in devices]
    return lax.ppermute(block, axis, route)


def short_conv(extended, short_filter, out_length):
    short_taps = short_filter.shape[0]
    running = jnp.zeros((out_length,) + extended.shape[1:], jnp.float32)
    for tap_index in range(short_taps):
        begin = short_taps - 1 - tap_index
        running = running + short_filter[tap_index][None] * extended[
            begin : begin + out_length
        ].astype(jnp.float32)
    return running


def body(
    token_ids, embed_table, norm_gain, in_weight, short_filter, long_filter, long_skip, out_weight
):
    tok_count = token_ids.shape[0]
    vocab_size = embed_table.shape[0]
    local_width = embed_table.shape[1]
    onehot = (token_ids[:, None] == jnp.arange(vocab_size, dtype=jnp.int32)[None, :]).astype(
        jnp.bfloat16
    )
    own_feats = jnp.dot(onehot, embed_table, preferred_element_type=jnp.float32).astype(
        jnp.bfloat16
    )
    features = lax.all_gather(own_feats, "tp", axis=1, tiled=True)
    widened = features.astype(jnp.float32)
    scaled = (
        widened
        * lax.rsqrt(jnp.mean(widened * widened, axis=1, keepdims=True) + 1e-06)
        * norm_gain[None, :]
    )
    normed = scaled.astype(jnp.bfloat16)
    projected = jnp.einsum(
        "td,dsc->tsc",
        normed,
        lax.all_gather(in_weight, "seq", axis=0, tiled=True),
        preferred_element_type=jnp.float32,
    ).astype(jnp.bfloat16)
    tap_count = long_filter.shape[1]
    short_taps = short_filter.shape[0]
    rim_rows = from_behind(projected[tok_count - short_taps + 1 :], "seq", 1)
    extended = jnp.concatenate([rim_rows, projected], axis=0)
    featured = short_conv(extended, short_filter, tok_count)
    queries = featured[:, 0]
    gated_kv = (featured[:, 1] * featured[:, 2]).astype(jnp.bfloat16)
    earlier = from_behind(gated_kv[tok_count - tap_count :], "seq", 1)
    product = jnp.concatenate([earlier, gated_kv], axis=0)
    groups_here = long_filter.shape[0]
    group_size = local_width // groups_here
    positions = jnp.arange(tap_count, dtype=jnp.int32)
    differ = positions[:, None, None] - positions[None, :, None]
    target = positions[None, None, :]
    near_pick = (differ == target).astype(jnp.float32)
    far_pick = (differ + tap_count == target).astype(jnp.float32)
    filter_f32 = long_filter.astype(jnp.float32)
    near_band = jnp.einsum("isj,gj->gis", near_pick, filter_f32).astype(jnp.bfloat16)
    far_band = jnp.einsum("isj,gj->gis", far_pick, filter_f32).astype(jnp.bfloat16)
    blocks = product.reshape(tok_count // tap_count + 1, tap_count, groups_here, group_size)
    convolved = jnp.einsum(
        "gis,bsgc->bigc", near_band, blocks[1:], preferred_element_type=jnp.float32
    )
    convolved = convolved + jnp.einsum(
        "gis,bsgc->bigc", far_band, blocks[:-1], preferred_element_type=jnp.float32
    )
    convolved = convolved.reshape(tok_count, local_width) + long_skip[None, :] * product[
        tap_count:
    ].astype(jnp.float32)
    gated = (queries * convolved).astype(jnp.bfloat16)
    partials = jnp.dot(
        gated,
        lax.all_gather(out_weight, "seq", axis=1, tiled=True),
        preferred_element_type=jnp.float32,
    )
    summed = lax.psum(partials.astype(jnp.bfloat16), "tp").astype(jnp.float32)
    own_share = lax.dynamic_slice_in_dim(summed, lax.axis_index("tp") * local_width, local_width, 1)
    return (own_feats.astype(jnp.float32) + own_share).astype(jnp.bfloat16)


def solution(mesh):
    placed = (
        P("seq"),
        P(None, "tp"),
        P(),
        P("seq", None, "tp"),
        P(None, None, "tp"),
        P("tp", None),
        P("tp"),
        P("tp", "seq"),
    )
    return jax.shard_map(
        body, mesh=mesh, in_specs=placed, out_specs=P("seq", "tp"), check_vma=False
    )
```

profile of v0, /device:TPU:1, one launch (start us, length us, event | category | flops | bytes accessed | tf_op | source)
XLA Modules:
  0.0 337.5 jit_solution(16231888260444834584)
XLA Ops:
  6.5 1.0 copy-done
  7.6 2.4 fusion.24
  10.1 0.7 all-gather.6.cloned.1.call-update
  10.8 0.7 all-gather.8.cloned.1.call-update
  11.6 1.2 fusion.38
  12.8 5.8 %fusion.3 = bf16[128,128,32]{1,2,0:T(8,128)(2,1)} fusion(s32[128,128]{1,0:T(8,128)S(1)} %iota_subtract_fusion, bf16[32,128]{1,0:T(8,128)(2,1)} %param.13), kind=kOutput, calls=%fused_computation.7 | convolution fusion | flops 136314880 | bytes 1122304 | tf_op jit(solution)/shard_map/isj,gj->gis/dot_general | solution.py:67
  18.6 5.1 %fusion.4 = bf16[128,128,32]{1,2,0:T(8,128)(2,1)} fusion(s32[128,128]{1,0:T(8,128)S(1)} %broadcast_add_fusion, bf16[32,128]{1,0:T(8,128)(2,1)S(1)} %copy-done.5), kind=kOutput, calls=%fused_computation.8 | convolution fusion | flops 136314880 | bytes 1122304 | tf_op jit(solution)/shard_map/isj,gj->gis/dot_general | solution.py:68
  23.7 40.8 %all-gather.4.cloned.1.call-done = bf16[1024,2048]{1,0:T(8,128)(2,1)} async-done(((bf16[1024,512]{1,0:T(8,128)(2,1)}), bf16[1024,2048]{1,0:T(8,128)(2,1)}) %all-gather.4.cloned.1.call-update) | async-done | bytes 4194320 | tf_op jit(solution)/shard_map/all_gather | solution.py:36
  64.6 3.1 fusion
  67.7 81.2 %all-gather.6.cloned.1.call-done = bf16[2048,3,512]{2,0,1:T(8,128)(2,1)} async-done(((bf16[32,3,512]{2,0,1:T(8,128)(2,1)}), bf16[2048,3,512]{2,0,1:T(8,128)(2,1)}) %all-gather.6.cloned.1.call-update) | async-done | bytes 6291472 | tf_op jit(solution)/shard_map/all_gather | solution.py:47
  148.8 10.5 %fusion.17 = bf16[1024,3,512]{2,0,1:T(8,128)(2,1)S(1)} fusion(bf16[2048,3,512]{2,0,1:T(8,128)(2,1)} %all-gather.6.cloned.1.call-done, bf16[1024,2048]{1,0:T(8,128)(2,1)} %all-gather.4.cloned.1.call-done, f32[2048]{0:T(1024)S(1)} %copy-done.6, f32[1024]{0:T(1024)S(1)} %add_rsqrt_fusion), kind=kOutput, calls=%fused_computation.31 | convolution fusion | flops 6452412416 | bytes 13643776 | tf_op jit(solution)/shard_map/td,dsc->tsc/dot_general | solution.py:44
  159.4 2.8 collective-permute-start
  162.2 0.9 collective-permute-done
  163.1 5.6 %multiply_add_fusion = f32[1024,3,512]{2,0,1:T(8,128)S(1)} fusion(bf16[1024,3,512]{2,0,1:T(8,128)(2,1)S(1)} %fusion.17, bf16[6,3,512]{2,0,1:T(8,128)(2,1)S(1)} %collective-permute-done, f32[3,512]{1,0:T(4,128)S(1)} %get-tuple-element.12, f32[3,512]{1,0:T(4,128)S(1)} %get-tuple-element.13, f32[3,512]{1,0:T(4,128)S(1)} %get-tuple-element.14, ...), kind=kLoop, calls=%fused_computation.14 | loop fusion | flops 59768832 | bytes 9498624 | tf_op jit(solution)/shard_map/add | solution.py:18
  168.7 2.7 copy-done.1
  171.3 0.4 fusion.20
  171.7 0.5 copy.12
  172.3 4.7 %collective-permute-start.1 = (bf16[128,512]{1,0:T(8,128)(2,1)S(1)}, bf16[128,512]{1,0:T(8,128)(2,1)S(1)}, u32[]{:S(2)}, u32[]{:S(2)}) collective-permute-start(bf16[128,512]{1,0:T(8,128)(2,1)S(1)} %slice_bitcast_fusion.1), channel_id=1, source_target_pairs={{0,4},{4,8},{8,12},{12,16},{16,20},{20,24},{24,28},{28,32},{32,36}... | collective-permute-start | bytes 393224 | tf_op jit(solution)/shard_map/ppermute | solution.py:10
  176.9 0.3 copy.29
  177.2 2.1 fusion.26
  179.3 0.4 fusion.42
  179.7 1.1 pad_maximum_fusion.1
  180.7 2.3 copy.14
  183.0 1.5 copy.30
  184.5 2.1 add_bitcast_fusion
  186.6 0.9 copy.16
  187.5 0.5 copy.52
  188.0 1.8 copy.17
  189.8 35.9 %all-gather.8.cloned.1.call-done = bf16[512,2048]{0,1:T(8,128)(2,1)} async-done(((bf16[512,32]{0,1:T(8,128)(2,1)}), bf16[512,2048]{0,1:T(8,128)(2,1)}) %all-gather.8.cloned.1.call-update) | async-done | bytes 2097168 | tf_op jit(solution)/shard_map/all_gather | solution.py:82
  225.7 7.6 %convolution_convert_fusion = bf16[1024,2048]{1,0:T(8,128)(2,1)} fusion(bf16[512,2048]{0,1:T(8,128)(2,1)} %all-gather.8.cloned.1.call-done, f32[1024,3,512]{2,0,1:T(8,128)} %copy-done.1, f32[1024,512]{1,0:T(8,128)} %copy.17, f32[512]{0:T(512)S(1)} %copy-done.7, bf16[1024,1,512]{2,0,1:T(8,128)(2,1)} %copy-done.3), kind=kOutput, calls=%fused_computation.21 | convolution fusion | flops 2152202240 | bytes 11536384 | tf_op jit(solution)/shard_map/dot_general | solution.py:80
  233.3 95.2 %all-reduce.2.cloned.1.call-done = bf16[1024,2048]{1,0:T(8,128)(2,1)} async-done(((bf16[1024,2048]{1,0:T(8,128)(2,1)}), bf16[1024,2048]{1,0:T(8,128)(2,1)}) %all-reduce.2.cloned.1.call-update) | async-done | bytes 4194320 | tf_op jit(solution)/shard_map/psum | solution.py:85
  328.5 2.5 add_convert_fusion
  (30 shorter events, 0.3 us)
Async XLA Ops:
  6.5 1.0 copy-start
  6.5 12.1 %copy-start.5 = (bf16[32,128]{1,0:T(8,128)(2,1)S(1)}, bf16[32,128]{1,0:T(8,128)(2,1)}, u32[]{:S(2)}) copy-start(bf16[32,128]{1,0:T(8,128)(2,1)} %param.13) | copy-start | bytes 24580
  6.5 58.0 %all-gather.4.cloned.1.call-start = ((), (), s32[]{:S(2)}) async-start(), calls=%async_computation | async-start | bytes 5242880 | tf_op jit(solution)/shard_map/all_gather | solution.py:36
  10.0 138.8 %all-gather.6.cloned.1.call-start = ((), (), s32[]{:S(2)}) async-start(), calls=%async_computation.1 | async-start | bytes 6389760 | tf_op jit(solution)/shard_map/all_gather | solution.py:47
  10.8 214.9 %all-gather.8.cloned.1.call-start = ((), (), s32[]{:S(2)}) async-start(), calls=%async_computation.2 | async-start | bytes 2129920 | tf_op jit(solution)/shard_map/all_gather | solution.py:82
  11.5 317.0 %all-reduce.2.cloned.1.call-start = ((), (), s32[]{:S(2)}) async-start(), calls=%async_computation.3 | async-start | bytes 8388608 | tf_op jit(solution)/shard_map/psum | solution.py:85
  12.8 136.0 %copy-start.6 = (f32[2048]{0:T(1024)S(1)}, f32[2048]{0:T(1024)}, u32[]{:S(2)}) copy-start(f32[2048]{0:T(1024)} %param.10) | copy-start | bytes 24580
  159.4 3.7 %collective-permute-start = (bf16[6,3,512]{2,0,1:T(8,128)(2,1)S(1)}, bf16[6,3,512]{2,0,1:T(8,128)(2,1)S(1)}, u32[]{:S(2)}, u32[]{:S(2)}) collective-permute-start(bf16[6,3,512]{2,0,1:T(8,128)(2,1)S(1)} %slice.86), channel_id=1, source_target_pairs={{0,4},{4,8},{8,12},{12,16},{16,20},{20,24},{24,28},{28,32},{32,36}... | collective-permute-start | bytes 55304 | tf_op jit(solution)/shard_map/ppermute | solution.py:10
  168.7 2.7 copy-start.1
  171.7 5.5 %copy-start.3 = (bf16[1024,1,512]{2,0,1:T(8,128)(2,1)}, bf16[1024,1,512]{2,0,1:T(8,128)(2,1)S(1)}, u32[]{:S(2)}) copy-start(bf16[1024,1,512]{2,0,1:T(8,128)(2,1)S(1)} %fusion.20) | copy-start | bytes 3145732
  172.2 7.1 %copy-start.2 = (f32[1024,3,512]{2,0,1:T(8,128)S(1)}, f32[1024,3,512]{2,0,1:T(8,128)}, u32[]{:S(2)}) copy-start(f32[1024,3,512]{2,0,1:T(8,128)} %copy-done.1) | copy-start | bytes 18874372
  172.3 7.4 %collective-permute-start.1 = (bf16[128,512]{1,0:T(8,128)(2,1)S(1)}, bf16[128,512]{1,0:T(8,128)(2,1)S(1)}, u32[]{:S(2)}, u32[]{:S(2)}) collective-permute-start(bf16[128,512]{1,0:T(8,128)(2,1)S(1)} %slice_bitcast_fusion.1), channel_id=1, source_target_pairs={{0,4},{4,8},{8,12},{12,16},{16,20},{20,24},{24,28},{28,32},{32,36}... | collective-permute-start | bytes 393224 | tf_op jit(solution)/shard_map/ppermute | solution.py:10
  186.6 39.1 %copy-start.7 = (f32[512]{0:T(512)S(1)}, f32[512]{0:T(512)}, u32[]{:S(2)}) copy-start(f32[512]{0:T(512)} %param.14) | copy-start | bytes 6148
  189.8 138.7 %copy-start.4 = (bf16[1024,512]{1,0:T(8,128)(2,1)S(1)}, bf16[1024,512]{1,0:T(8,128)(2,1)}, u32[]{:S(2)}) copy-start(bf16[1024,512]{1,0:T(8,128)(2,1)} %fusion.24) | copy-start | bytes 3145732
Sparse Core Ops, SparseCore 0:
  10.1 54.3 all-gather.3
  67.4 81.3 all-gather.5
  151.6 74.0 all-gather.7
  233.4 94.9 all-reduce.1
where the time goes:
time: 338 us; the launch traced here: 337 us
  waiting for transfers between devices  255 us (75%)
  matrix products  35.6 us (11%)
  between operations  13.3 us (4%)
  other arithmetic  12.9 us (4%)
  local copies, waits for them, and re-layouts  12.7 us (4%)
  starting transfers between devices  7.53 us (2%)
    psum x1, waiting for transfers between devices, body(): summed = lax.psum(partials.astype(jnp.bfloat16), 'tp').astype(jnp.float32)  95.2 us
    all_gather x1, waiting for transfers between devices, body(): lax.all_gather(in_weight, 'seq', axis=0, tiled=True)  81.2 us
    all_gather x1, waiting for transfers between devices, body(): features = lax.all_gather(own_feats, 'tp', axis=1, tiled=True)  40.8 us
    all_gather x1, waiting for transfers between devices, body(): lax.all_gather(out_weight, 'seq', axis=1, tiled=True)  35.9 us
    dot_general x1, matrix products, body(): jnp.einsum('td,dsc->tsc', normed, lax.all_gather(in_weight, 'seq', axis=0...  10.5 us
    dot_general x1, matrix products, body(): jnp.dot(gated, lax.all_gather(out_weight, 'seq', axis=1, tiled=True), pre...  7.59 us
    ppermute x2, starting transfers between devices, from_behind(): return lax.ppermute(block, axis, route)  7.41 us
  transfers between devices with their start and end apart: 6, of which 5 were waited for; matrix products, arithmetic and copies ran while one was open for 13% of the time, Pallas kernels for 0%

commit v1 on v0

v1 whole, which is shorter than its diff:
```python
import functools

import jax
import jax.numpy as jnp
from jax import lax
from jax.experimental import pallas as pl
from jax.experimental.pallas import tpu as pltpu
from jax.sharding import PartitionSpec as P

MESH = pl.DeviceIdType.MESH
BF16 = jnp.bfloat16
F32 = jnp.float32
NX, NZ, NC, NY = 4, 8, 2, 4
LINE = NZ * NC
TILES = 10


def kernel(
    tok_ref, emb_ref, gain_ref, w_ref, wo_ref, sf_ref, lf_ref, out_ref,
    tprev, sf2, lf2, wl, e4, tt, wt, g4, oneh, band, taps, proj, acc,
    tok_s, tok_r, fil_s, fil_r, s1_s, s1_r, s2_s, s2_r, e_s, e_r, wo_s, wo_r, t2_s, t2_r,
    ax_s, ax_r, az_s, az_r, ad_s, ad_r, g_s, g_r,
):
    s = lax.axis_index("seq")
    y = lax.axis_index("tp")
    zc = lax.rem(s, LINE)
    x = s // LINE
    z = zc // NC
    c = lax.rem(zc, NC)
    sign = 1 - 2 * c
    far = lax.rem(y + 2, NY)
    turned = y * LINE + zc

    def at_x(q):
        return (lax.rem(x + q, NX) * LINE + zc, y)

    def at_y(q):
        return (s, lax.rem(y + q, NY))

    def at_z(q):
        return (x * LINE + lax.rem(z + q + NZ, NZ) * NC + c, y)

    mate = (s + sign, y)
    after = (lax.rem(s + 1, NX * LINE), y)
    before = (lax.rem(s + NX * LINE - 1, NX * LINE), y)

    sent = []

    def copy(src, dst, ss, rs, dev):
        return pltpu.make_async_remote_copy(
            src_ref=src, dst_ref=dst, send_sem=ss, recv_sem=rs, device_id=dev, device_id_type=MESH
        )

    def send(*args):
        one = copy(*args)
        one.start()
        sent.append(one)

    hello = pltpu.get_barrier_semaphore()
    greeted = 0
    for r in range(1, LINE):
        pl.semaphore_signal(
            hello, inc=1, device_id=(x * LINE + lax.rem(zc + r, LINE), y), device_id_type=MESH
        )
        greeted += 1
    for r in range(1, NX):
        pl.semaphore_signal(hello, inc=1, device_id=at_x(r), device_id_type=MESH)
        pl.semaphore_signal(hello, inc=1, device_id=at_y(r), device_id_type=MESH)
        greeted += 2
    pl.semaphore_signal(hello, inc=1, device_id=after, device_id_type=MESH)
    pl.semaphore_signal(hello, inc=1, device_id=before, device_id_type=MESH)
    greeted += 2

    @pl.when(x != y)
    def _():
        pl.semaphore_signal(hello, inc=1, device_id=(turned, x), device_id_type=MESH)

    pl.semaphore_wait(hello, greeted + jnp.where(x == y, 0, 1))

    for r in range(1, LINE):
        other = lax.rem(zc + r, LINE)
        send(w_ref.at[other], wl.at[x, zc], s1_s.at[r - 1], s1_r.at[r - 1], (x * LINE + other, y))
    for r in range(1, NY):
        send(
            emb_ref.at[pl.ds(pl.multiple_of(x * 128, 128), 128)],
            e4.at[y], e_s.at[r - 1], e_r.at[r - 1], at_y(r),
        )
    send(tok_ref, tprev, tok_s, tok_r, after)
    send(sf_ref, sf2, fil_s.at[0], fil_r.at[0], at_y(2))
    send(lf_ref, lf2, fil_s.at[1], fil_r.at[1], at_y(2))

    @pl.when(x != y)
    def _():
        copy(wo_ref, wt.at[zc, y], wo_s, wo_r, (turned, x)).start()

    @pl.when(x == y)
    def _():
        wt[zc, x] = wo_ref[...]

    wl[x, zc] = w_ref[zc]
    e4[y] = emb_ref[pl.ds(pl.multiple_of(x * 128, 128), 128), :]

    ids = lax.broadcasted_iota(jnp.int32, (512, 128), 0)
    for tile in range(8):
        row = tok_ref[tile : tile + 1, :]
        oneh[:, (tile + 2) * 128 : (tile + 3) * 128] = (
            jnp.where(ids == row, 1.0, 0.0).astype(BF16)
        )

    above = lax.broadcasted_iota(jnp.int32, (128, 128), 1) >= lax.broadcasted_iota(
        jnp.int32, (128, 128), 0
    )

    def bands(which, filters):
        def build(g, carry):
            rows = jnp.broadcast_to(filters[pl.ds(g, 1), :], (128, 128))
            turnedrows = pltpu.roll(rows, 0, 1, stride=1, stride_axis=0)
            band[which, g, 0:128, :] = jnp.where(above, 0.0, turnedrows).astype(BF16)
            band[which, g, 128:256, :] = jnp.where(above, turnedrows, 0.0).astype(BF16)
            return carry

        lax.fori_loop(0, 32, build, 0)

    def columns(which, filters):
        for p in range(4):
            for part in range(3):
                taps[which, p, part] = filters[p, part].T

    columns(0, sf_ref)

    for r in range(1, LINE):
        copy(w_ref.at[0], wl.at[x, lax.rem(zc + LINE - r, LINE)], s1_s.at[r - 1], s1_r.at[r - 1], mate).wait_recv()
    for r in range(1, NX):
        send(wl.at[x], wl.at[x], s2_s.at[r - 1], s2_r.at[r - 1], at_x(r))
    for r in range(1, NY):
        copy(e4.at[0], e4.at[lax.rem(y + NY - r, NY)], e_s.at[r - 1], e_r.at[r - 1], mate).wait_recv()

    total = jnp.zeros((128, 1), F32)
    for k in range(NY):
        piece = e4[k].astype(F32)
        total = total + jnp.sum(piece * piece, axis=1, keepdims=True)
    scale = lax.rsqrt(total * (1.0 / 2048) + 1e-06)
    normed = [
        (e4[k].astype(F32) * scale * gain_ref[k]).astype(BF16) for k in range(NY)
    ]
    for r in range(1, NX):
        copy(wl.at[0], wl.at[lax.rem(x + NX - r, NX)], s2_s.at[r - 1], s2_r.at[r - 1], mate).wait_recv()
    table = jnp.zeros((128, 128), F32)
    for k in range(NX):
        table = table + jnp.dot(
            normed[k], wl[k].reshape(512, 128), preferred_element_type=F32
        )
    tt[0, zc, x] = table.T[0:96].astype(BF16)

    class Gather:
        def __init__(self, n, buf):
            self.n, self.buf = n, buf

        def xsend(self):
            for q in range(1, NX):
                here = self.buf.at[zc, x]
                send(here, here, ax_s.at[self.n, q - 1], ax_r.at[self.n, q - 1], at_x(q))

        def zsend(self, way, step, piece):
            hop = sign if way == 0 else -sign
            block = lax.rem(z - hop * (step - 1) + NZ, NZ) * NC + c
            here = self.buf.at[block, lax.rem(x + NX - piece, NX)]
            at = (self.n, way, step - 1, piece)
            send(here, here, az_s.at[at], az_r.at[at], at_z(hop))

        def zwait(self, way, step, piece):
            hop = sign if way == 0 else -sign
            block = lax.rem(z - hop * step + NZ, NZ) * NC + c
            here = self.buf.at[block, lax.rem(x + NX - piece, NX)]
            at = (self.n, way, step - 1, piece)
            copy(here, here, az_s.at[at], az_r.at[at], mate).wait_recv()
            return block

        def dsend(self, slot, block):
            here = self.buf.at[block]
            send(here, here, ad_s.at[self.n, slot], ad_r.at[self.n, slot], mate)

        def dwait(self, slot, block):
            here = self.buf.at[block]
            copy(here, here, ad_s.at[self.n, slot], ad_r.at[self.n, slot], mate).wait_recv()

        def first(self):
            self.xsend()
            for piece in range(NX):
                if piece:
                    there = self.buf.at[zc, lax.rem(x + NX - piece, NX)]
                    copy(there, there, ax_s.at[self.n, piece - 1], ax_r.at[self.n, piece - 1], mate).wait_recv()
                self.zsend(0, 1, piece)
                self.zsend(1, 1, piece)
            self.dsend(0, zc)

        def step(self, i):
            blocks = []
            for piece in range(NX):
                for way in range(2):
                    last = 4 if way == 0 else 3
                    if i <= last:
                        block = self.zwait(way, i, piece)
                        if piece == 0:
                            blocks.append(block)
                        if i < last:
                            self.zsend(way, i + 1, piece)
            for way, block in enumerate(blocks):
                self.dsend(2 * i - 1 + way, block)

        def settle(self, i):
            if i == 1:
                self.dwait(0, zc + sign)
            for way in range(2):
                last = 4 if way == 0 else 3
                if i <= last:
                    hop = -sign if way == 0 else sign
                    block = lax.rem(z - hop * i + NZ, NZ) * NC + (1 - c)
                    self.dwait(2 * i - 1 + way, block)

    table_own = Gather(0, tt.at[0])
    table_far = Gather(1, tt.at[1])
    outw = Gather(2, wt)

    send(tt.at[0, zc, x], tt.at[1, zc, x], t2_s, t2_r, at_y(2))
    table_own.first()
    bands(0, lf_ref)

    copy(tok_ref, tprev, tok_s, tok_r, mate).wait_recv()
    for tile in range(2):
        row = tprev[tile + 6 : tile + 7, :]
        row = jnp.where(s == 0, -1, row)
        oneh[:, tile * 128 : (tile + 1) * 128] = jnp.where(ids == row, 1.0, 0.0).astype(BF16)

    pair0 = z // 2
    even = 1 - 2 * lax.rem(z, 2)

    def pair(i):
        move = (0, -even, even, 2)[i - 1]
        return lax.rem(pair0 + move + 4, 4)

    lane = lax.broadcasted_iota(jnp.int32, (16, 128), 1)

    def fir(rows, tap, first):
        f = [jnp.broadcast_to(tap[:, n : n + 1], (16, 128)) for n in range(7)]
        outs = {}
        for tile in range(first - 1, TILES):
            cur = proj[pl.ds(rows, 16), tile * 128 : (tile + 1) * 128]
            turn = [pltpu.roll(cur, n, 1) for n in (1, 2, 3)]
            if tile >= first:
                lag = [jnp.where(lane < n + 1, old[n], turn[n]) for n in range(3)]
            else:
                lag = turn
            late = f[4] * cur + f[5] * lag[0] + f[6] * lag[1]
            late = pltpu.roll(late, 4, 1)
            if tile >= first:
                outs[tile] = (
                    f[0] * cur + f[1] * lag[0] + f[2] * lag[1] + f[3] * lag[2]
                    + jnp.where(lane < 4, oldlate, late)
                )
            old, oldlate = turn, late
        return outs

    def block(which, k, p):
        left = jnp.concatenate(
            [tt[which, pl.ds(4 * p, 4), b].reshape(384, 128) for b in range(NX)], axis=1
        )
        for n in range(5):
            proj[:, n * 256 : (n + 1) * 256] = jnp.dot(
                left, oneh[:, n * 256 : (n + 1) * 256], preferred_element_type=F32
            )

        def group(g, carry):
            ch = pl.multiple_of(g * 16, 16)
            base = (g // 2) * 96 + lax.rem(g, 2) * 16
            tap = [taps[which, p, part, pl.ds(ch, 16), :] for part in range(3)]
            key = fir(pl.multiple_of(base + 32, 16), tap[1], 1)
            val = fir(pl.multiple_of(base + 64, 16), tap[2], 1)
            prod = {tile: (key[tile] * val[tile]).astype(BF16) for tile in key}
            rows = jnp.concatenate(
                [jnp.concatenate([prod[t - 1], prod[t]], axis=1) for t in range(2, TILES)], axis=0
            )
            conv = jnp.dot(rows, band[which, 8 * p + g], preferred_element_type=F32)
            query = fir(pl.multiple_of(base, 16), tap[0], 2)
            skip = jnp.broadcast_to(tap[0][:, 7:8], (16, 128))
            for t in range(2, TILES):
                whole = conv[(t - 2) * 16 : (t - 1) * 16] + skip * prod[t].astype(F32)
                g4[k, p, pl.ds(ch, 16), (t - 2) * 128 : (t - 1) * 128] = (
                    query[t] * whole
                ).astype(BF16)
            return carry

        lax.fori_loop(0, 8, group, 0)

    def gsend(i):
        p = pair(i)
        here = g4.at[y, p]
        for way, q in ((0, 1), (1, 3)):
            send(here, here, g_s.at[way, i - 1], g_r.at[way, i - 1], at_y(q))

    def gwait(i):
        p = pair(i)
        for way, q in ((0, 3), (1, 1)):
            here = g4.at[lax.rem(y + q, NY), p]
            copy(here, here, g_s.at[way, i - 1], g_r.at[way, i - 1], mate).wait_recv()

    def own(i):
        table_own.settle(i)
        block(0, y, pair(i))
        gsend(i)

    def others(i):
        table_far.settle(i)
        block(1, far, pair(i))

    table_own.step(1)
    own(1)
    table_own.step(2)
    copy(tt.at[0, zc, x], tt.at[1, zc, x], t2_s, t2_r, mate).wait_recv()
    table_far.first()
    own(2)
    table_own.step(3)
    table_far.step(1)

    @pl.when(x != y)
    def _():
        copy(wo_ref, wt.at[zc, x], wo_s, wo_r, mate).wait()

    outw.first()
    own(3)
    table_own.step(4)
    table_far.step(2)
    outw.step(1)
    own(4)
    table_far.step(3)
    outw.step(2)
    for n in range(2):
        ref = (sf2, lf2)[n]
        copy(ref, ref, fil_s.at[n], fil_r.at[n], mate).wait_recv()
    columns(1, sf2)
    bands(1, lf2)
    others(1)
    table_far.step(4)
    outw.step(3)
    others(2)
    outw.step(4)
    others(3)
    others(4)
    for i in range(1, 5):
        outw.settle(i)

    def project(ks, n):
        sums = None
        for k in ks:
            left = jnp.concatenate(
                [wt[pl.ds(4 * n, 4), k, p].reshape(128, 128) for p in range(4)], axis=1
            )
            term = jnp.dot(left, g4[k].reshape(512, 1024), preferred_element_type=F32)
            sums = term if sums is None else sums + term
        return sums

    def near(n, carry):
        cols = pl.ds(pl.multiple_of(n * 128, 128), 128)
        resid = lax.dot_general(
            emb_ref[:, cols], oneh[:, 256:], (((0,), (0,)), ((), ())), preferred_element_type=F32
        )
        acc[cols, :] = resid + project((y, far), n)
        return carry

    lax.fori_loop(0, 4, near, 0)
    for i in range(1, 5):
        gwait(i)

    def rest(n, carry):
        rows = pl.ds(pl.multiple_of(n * 128, 128), 128)
        ks = (lax.rem(y + 1, NY), lax.rem(y + 3, NY))
        out_ref[rows, :] = (acc[rows, :] + project(ks, n)).astype(BF16)
        return carry

    lax.fori_loop(0, 4, rest, 0)
    for one in sent:
        one.wait_send()


def body(
    token_ids, embed_table, norm_gain, in_weight, short_filter, long_filter, long_skip, out_weight
):
    tok = token_ids.reshape(8, 128)
    gain = norm_gain.reshape(4, 1, 512)
    w = in_weight.reshape(32, 3, 16, 32).transpose(2, 0, 1, 3).reshape(16, 32, 96)
    w = jnp.pad(w, ((0, 0), (0, 0), (0, 32)))
    wo = out_weight.T.reshape(32, 4, 128).transpose(1, 0, 2)
    skip = jnp.broadcast_to(long_skip[None, None, :], (1, 3, 512))
    sf = jnp.concatenate([short_filter, skip], axis=0)
    sf = sf.reshape(8, 3, 4, 128).transpose(2, 1, 0, 3)
    lf = long_filter.astype(F32)
    vmem = pl.BlockSpec(memory_space=pltpu.VMEM)
    dma = pltpu.SemaphoreType.DMA
    out = pl.pallas_call(
        kernel,
        out_shape=jax.ShapeDtypeStruct((512, 1024), BF16),
        in_specs=[vmem] * 7,
        out_specs=vmem,
        scratch_shapes=[
            pltpu.VMEM((8, 128), jnp.int32),
            pltpu.VMEM((4, 3, 8, 128), F32),
            pltpu.VMEM((32, 128), F32),
            pltpu.VMEM((NX, LINE, 32, 128), BF16),
            pltpu.VMEM((NY, 128, 512), BF16),
            pltpu.VMEM((2, LINE, NX, 96, 128), BF16),
            pltpu.VMEM((LINE, NX, 4, 32, 128), BF16),
            pltpu.VMEM((NY, 4, 128, 1024), BF16),
            pltpu.VMEM((512, TILES * 128), BF16),
            pltpu.VMEM((2, 32, 256, 128), BF16),
            pltpu.VMEM((2, 4, 3, 128, 8), F32),
            pltpu.VMEM((384, TILES * 128), F32),
            pltpu.VMEM((512, 1024), F32),
            dma, dma, dma((2,)), dma((2,)), dma((LINE - 1,)), dma((LINE - 1,)),
            dma((3,)), dma((3,)), dma((3,)), dma((3,)), dma, dma, dma, dma,
            dma((3, 3)), dma((3, 3)), dma((3, 2, 4, 4)), dma((3, 2, 4, 4)),
            dma((3, 8)), dma((3, 8)), dma((2, 4)), dma((2, 4)),
        ],
        compiler_params=pltpu.CompilerParams(
            collective_id=0, has_side_effects=True, vmem_limit_bytes=60 * 2**20
        ),
    )(tok, embed_table, gain, w, wo, sf, lf)
    return out.T


def solution(mesh):
    placed = (
        P("seq"),
        P(None, "tp"),
        P(),
        P("seq", None, "tp"),
        P(None, None, "tp"),
        P("tp", None),
        P("tp"),
        P("tp", "seq"),
    )
    return jax.shard_map(
        body, mesh=mesh, in_specs=placed, out_specs=P("seq", "tp"), check_vma=False
    )
```

time: 338 us -> 107 us (0.32)
  waiting for transfers between devices: 255 us -> 0 us
  Pallas kernels: 0 us -> 101 us
  matrix products: 35.6 us -> 0 us
  between operations: 13.3 us -> 0.04 us
  other arithmetic: 12.9 us -> 1.22 us
  local copies, waits for them, and re-layouts: 12.7 us -> 5.07 us
  starting transfers between devices: 7.53 us -> 0 us
    all_gather x3 -> x0, waiting for transfers between devices: 158 us -> none  [the longest x1 81.2 us: body(): lax.all_gather(in_weight, 'seq', axis=0, tiled=True)]
    pallas_call x0 -> x1, Pallas kernels: none -> 101 us  [body(): pl.pallas_call(kernel, out_shape=jax.ShapeDtypeStruct((512, 1024), BF16),...]
    psum x1 -> x0, waiting for transfers between devices: 95.2 us -> none  [body(): summed = lax.psum(partials.astype(jnp.bfloat16), 'tp').astype(jnp.float32)]
    dot_general x7 -> x0, matrix products: 35.6 us -> none  [the longest x1 10.5 us: body(): jnp.einsum('td,dsc->tsc', normed, lax.all_gather(in_weight, 'seq', axis=0...]
    ppermute x2 -> x0, starting transfers between devices: 7.41 us -> none  [from_behind(): return lax.ppermute(block, axis, route)]
    add x2 -> x0, other arithmetic: 5.61 us -> none  [the longest x1 5.6 us: short_conv(): running + short_filter[tap_index][None] * extended[begin:begin + out_leng...]
    unnamed x23 -> x10, local copies, waits for them, and re-layouts: 5.97 us -> 0.72 us
    slice x4 -> x0, local copies, waits for them, and re-layouts: 3.49 us -> none  [the longest x1 2.27 us: body(): blocks[:-1]]
  transfers between devices with their start and end apart: 6 -> 0, of which waited for: 5 -> 0; matrix products, arithmetic and copies ran while one was open for 13% -> 0% of each run, Pallas kernels for 0% -> 0%
where the time goes in v1:
time: 107 us
  Pallas kernels  101 us (94%)
  local copies, waits for them, and re-layouts  5.07 us (5%)
  other arithmetic  1.22 us (1%)
    pallas_call x1, Pallas kernels, body(): pl.pallas_call(kernel, out_shape=jax.ShapeDtypeStruct((512, 1024), BF16),...  101 us
    transpose x1, local copies, waits for them, and re-layouts, body(): return out.T  2.28 us

profile of v1, /device:TPU:1, one launch (start us, length us, event | category | flops | bytes accessed | tf_op | source)
XLA Modules:
  0.0 107.0 jit_solution(5220726638869106689)
XLA Ops:
  0.0 0.0 copy-start
  0.0 0.0 copy-start.4
  0.0 0.0 copy-start.3
  0.0 0.7 copy-done.4
  0.7 0.0 copy-start.2
  0.7 0.0 copy-done.3
  0.7 0.0 copy-start.1
  0.7 0.6 convert_element_type.5.lf_ref
  1.3 0.0 copy-done
  1.3 0.6 bitcast_bitcast_fusion.1.wo_ref
  1.9 0.0 copy-done.2
  1.9 0.6 bitcast_bitcast_fusion.sf_ref
  2.6 0.0 copy-done.1
  2.6 0.2 reshape.23
  2.8 0.3 copy.20
  3.1 0.2 reshape.24
  3.4 0.7 pad.4.w_ref
  4.0 100.6 %shard_map.82 = bf16[512,1024]{1,0:T(8,128)(2,1)} custom-call(s32[8,128]{1,0:T(8,128)} %bitcast.26, bf16[512,512]{1,0:T(8,128)(2,1)} %emb_ref.1, f32[4,1,512]{2,1,0:T(1,128)} %bitcast.25, bf16[16,32,128]{2,1,0:T(8,128)(2,1)} %pad.4.w_ref, bf16[4,32,128]{2,1,0:T(8,128)(2,1)} %bitcast_bitcast_fusion.1.wo_ref, f32[4,3,8,128]{3,2,1,0:T(8,128)} %bitcast_bitcast_fusion.sf_ref, ...), custom_call_target="tpu_custom_call" | custom-call | tf_op jit(solution)/shard_map/pallas_call | solution.py:399
  104.7 2.3 %copy.14 = bf16[1024,512]{1,0:T(8,128)(2,1)} copy(bf16[1024,512]{0,1:T(8,128)(2,1)} %bitcast.23) | data formatting | bytes 2097152 | tf_op jit(solution)/shard_map/transpose | solution.py:427
  (1 shorter events, 0.0 us)
Async XLA Ops:
  0.0 1.3 %copy-start = (bf16[512,32]{0,1:T(8,128)(2,1)S(1)}, bf16[512,32]{0,1:T(8,128)(2,1)}, u32[]{:S(2)}) copy-start(bf16[512,32]{0,1:T(8,128)(2,1)} %param.15) | copy-start | bytes 98308
  0.0 0.7 copy-start.4
  0.0 0.7 copy-start.3
  0.7 1.2 %copy-start.2 = (f32[7,3,512]{2,0,1:T(8,128)S(1)}, f32[7,3,512]{2,0,1:T(8,128)}, u32[]{:S(2)}) copy-start(f32[7,3,512]{2,0,1:T(8,128)} %param.12) | copy-start | bytes 129028
  0.7 1.8 %copy-start.1 = (bf16[32,3,512]{2,0,1:T(8,128)(2,1)S(1)}, bf16[32,3,512]{2,0,1:T(8,128)(2,1)}, u32[]{:S(2)}) copy-start(bf16[32,3,512]{2,0,1:T(8,128)(2,1)} %param.11) | copy-start | bytes 294916

commit v2 on v1

--- a/solution.py
+++ b/solution.py
@@ -16,10 +16,10 @@
 
 
 def kernel(
-    tok_ref, emb_ref, gain_ref, w_ref, wo_ref, sf_ref, lf_ref, out_ref,
-    tprev, sf2, lf2, wl, e4, tt, wt, g4, oneh, band, taps, proj, acc,
+    tok_ref, emb_ref, gain_ref, w_ref, wo_ref, short_ref, skip_ref, long_ref, out_ref,
+    tprev, sf, lf, wsend, wosend, wl, e4, tt, wt, g4, oneh, band, taps, proj, acc, stage,
     tok_s, tok_r, fil_s, fil_r, s1_s, s1_r, s2_s, s2_r, e_s, e_r, wo_s, wo_r, t2_s, t2_r,
-    ax_s, ax_r, az_s, az_r, ad_s, ad_r, g_s, g_r,
+    ax_s, ax_r, az_s, az_r, ad_s, ad_r, g_s, g_r, out_s,
 ):
     s = lax.axis_index("seq")
     y = lax.axis_index("tp")
@@ -75,30 +75,28 @@
     def _():
         pl.semaphore_signal(hello, inc=1, device_id=(turned, x), device_id_type=MESH)
 
-    pl.semaphore_wait(hello, greeted + jnp.where(x == y, 0, 1))
-
-    for r in range(1, LINE):
-        other = lax.rem(zc + r, LINE)
-        send(w_ref.at[other], wl.at[x, zc], s1_s.at[r - 1], s1_r.at[r - 1], (x * LINE + other, y))
-    for r in range(1, NY):
-        send(
-            emb_ref.at[pl.ds(pl.multiple_of(x * 128, 128), 128)],
-            e4.at[y], e_s.at[r - 1], e_r.at[r - 1], at_y(r),
-        )
-    send(tok_ref, tprev, tok_s, tok_r, after)
-    send(sf_ref, sf2, fil_s.at[0], fil_r.at[0], at_y(2))
-    send(lf_ref, lf2, fil_s.at[1], fil_r.at[1], at_y(2))
-
-    @pl.when(x != y)
-    def _():
-        copy(wo_ref, wt.at[zc, y], wo_s, wo_r, (turned, x)).start()
+    lane32 = lax.broadcasted_iota(jnp.int32, (32, 128), 1) // 32
+    for p in range(4):
+        chunk = [w_ref[part, :, p * 128 : (p + 1) * 128] for part in range(3)]
+        for n in range(4):
+            moved = [
+                chunk[part] if part == n else pltpu.roll(chunk[part], (part - n) % 4 * 32, 1)
+                for part in range(3)
+            ]
+            wsend[4 * p + n] = jnp.where(
+                lane32 == 0, moved[0], jnp.where(lane32 == 1, moved[1], moved[2])
+            )
+        wosend[p] = wo_ref[:, p * 128 : (p + 1) * 128]
+        for part in range(3):
+            sf[0, p, part, 0:7, :] = short_ref[part, :, p * 128 : (p + 1) * 128]
+            sf[0, p, part, 7:8, :] = skip_ref[:, p * 128 : (p + 1) * 128]
+    lf[0] = long_ref[...].astype(F32)
+    wl[x, zc] = wsend[zc]
+    e4[y] = emb_ref[pl.ds(pl.multiple_of(x * 128, 128), 128), :]
 
     @pl.when(x == y)
     def _():
-        wt[zc, x] = wo_ref[...]
-
-    wl[x, zc] = w_ref[zc]
-    e4[y] = emb_ref[pl.ds(pl.multiple_of(x * 128, 128), 128), :]
+        wt[zc, x] = wosend[...]
 
     ids = lax.broadcasted_iota(jnp.int32, (512, 128), 0)
     for tile in range(8):
@@ -111,29 +109,68 @@
         jnp.int32, (128, 128), 0
     )
 
-    def bands(which, filters):
+    def bands(which):
         def build(g, carry):
-            rows = jnp.broadcast_to(filters[pl.ds(g, 1), :], (128, 128))
-            turnedrows = pltpu.roll(rows, 0, 1, stride=1, stride_axis=0)
-            band[which, g, 0:128, :] = jnp.where(above, 0.0, turnedrows).astype(BF16)
-            band[which, g, 128:256, :] = jnp.where(above, turnedrows, 0.0).astype(BF16)
+            rows = jnp.broadcast_to(lf[which, pl.ds(g, 1), :], (128, 128))
+            moved = pltpu.roll(rows, 0, 1, stride=1, stride_axis=0)
+            band[which, g, 0:128, :] = jnp.where(above, 0.0, moved).astype(BF16)
+            band[which, g, 128:256, :] = jnp.where(above, moved, 0.0).astype(BF16)
             return carry
 
         lax.fori_loop(0, 32, build, 0)
 
-    def columns(which, filters):
+    def columns(which):
         for p in range(4):
             for part in range(3):
-                taps[which, p, part] = filters[p, part].T
-
-    columns(0, sf_ref)
+                taps[which, p, part] = sf[which, p, part].T
+
+    columns(0)
+    bands(0)
+    pl.semaphore_wait(hello, greeted + jnp.where(x == y, 0, 1))
+
+    half = pl.ds(pl.multiple_of(64 * c, 64), 64)
+    other = pl.ds(pl.multiple_of(64 - 64 * c, 64), 64)
+    for r in (8, 7, 9, 6, 10, 5, 11, 4, 12, 3, 13, 2, 14, 1, 15):
+        to = lax.rem(zc + r, LINE)
+        send(wsend.at[to], wl.at[x, zc], s1_s.at[r - 1], s1_r.at[r - 1], (x * LINE + to, y))
+    for r in (2, 1, 3):
+        send(
+            emb_ref.at[pl.ds(pl.multiple_of(x * 128 + 64 * c, 64), 64)],
+            e4.at[y, half], e_s.at[0, r - 1], e_r.at[0, r - 1], at_y(r),
+        )
+    send(tok_ref, tprev, tok_s, tok_r, after)
+    send(sf.at[0], sf.at[1], fil_s.at[0], fil_r.at[0], at_y(2))
+    send(lf.at[0], lf.at[1], fil_s.at[1], fil_r.at[1], at_y(2))
+
+    @pl.when(x != y)
+    def _():
+        copy(wosend, wt.at[zc, y], wo_s, wo_r, (turned, x)).start()
 
     for r in range(1, LINE):
-        copy(w_ref.at[0], wl.at[x, lax.rem(zc + LINE - r, LINE)], s1_s.at[r - 1], s1_r.at[r - 1], mate).wait_recv()
-    for r in range(1, NX):
-        send(wl.at[x], wl.at[x], s2_s.at[r - 1], s2_r.at[r - 1], at_x(r))
-    for r in range(1, NY):
-        copy(e4.at[0], e4.at[lax.rem(y + NY - r, NY)], e_s.at[r - 1], e_r.at[r - 1], mate).wait_recv()
+        here = wl.at[x, lax.rem(zc + LINE - r, LINE)]
+        copy(here, here, s1_s.at[r - 1], s1_r.at[r - 1], mate).wait_recv()
+
+    parts = (pl.ds(0, 8), pl.ds(8, 8))
+    for way, q in ((0, 1), (1, 3)):
+        for n in (way, 1 - way):
+            here = wl.at[x, parts[n]]
+            send(here, here, s2_s.at[way, n], s2_r.at[way, n], at_x(q))
+    for r in (1, 3, 2):
+        here = e4.at[lax.rem(y + NY - r, NY), half]
+        copy(here, here, e_s.at[0, r - 1], e_r.at[0, r - 1], mate).wait_recv()
+        send(here, here, e_s.at[1, r - 1], e_r.at[1, r - 1], mate)
+    for way, q in ((0, 1), (1, 3)):
+        here = wl.at[lax.rem(x + NX - q, NX), parts[way]]
+        copy(here, here, s2_s.at[way, way], s2_r.at[way, way], mate).wait_recv()
+        send(here, here, s2_s.at[2, way], s2_r.at[2, way], at_x(q))
+    for n in range(2):
+        ref = (sf, lf)[n].at[1]
+        copy(ref, ref, fil_s.at[n], fil_r.at[n], mate).wait_recv()
+    columns(1)
+    bands(1)
+    for r in (1, 3, 2):
+        here = e4.at[lax.rem(y + NY - r, NY), other]
+        copy(here, here, e_s.at[1, r - 1], e_r.at[1, r - 1], mate).wait_recv()
 
     total = jnp.zeros((128, 1), F32)
     for k in range(NY):
@@ -143,8 +180,18 @@
     normed = [
         (e4[k].astype(F32) * scale * gain_ref[k]).astype(BF16) for k in range(NY)
     ]
-    for r in range(1, NX):
-        copy(wl.at[0], wl.at[lax.rem(x + NX - r, NX)], s2_s.at[r - 1], s2_r.at[r - 1], mate).wait_recv()
+    copy(tok_ref, tprev, tok_s, tok_r, mate).wait_recv()
+    for tile in range(2):
+        row = tprev[tile + 6 : tile + 7, :]
+        row = jnp.where(s == 0, -1, row)
+        oneh[:, tile * 128 : (tile + 1) * 128] = jnp.where(ids == row, 1.0, 0.0).astype(BF16)
+
+    for way, q in ((0, 1), (1, 3)):
+        here = wl.at[lax.rem(x + NX - q, NX), parts[1 - way]]
+        copy(here, here, s2_s.at[way, 1 - way], s2_r.at[way, 1 - way], mate).wait_recv()
+    for way in range(2):
+        here = wl.at[lax.rem(x + 2, NX), parts[way]]
+        copy(here, here, s2_s.at[2, way], s2_r.at[2, way], mate).wait_recv()
     table = jnp.zeros((128, 128), F32)
     for k in range(NX):
         table = table + jnp.dot(
@@ -185,7 +232,6 @@
             copy(here, here, ad_s.at[self.n, slot], ad_r.at[self.n, slot], mate).wait_recv()
 
         def first(self):
-            self.xsend()
             for piece in range(NX):
                 if piece:
                     there = self.buf.at[zc, lax.rem(x + NX - piece, NX)]
@@ -223,14 +269,14 @@
     outw = Gather(2, wt)
 
     send(tt.at[0, zc, x], tt.at[1, zc, x], t2_s, t2_r, at_y(2))
+    table_own.xsend()
     table_own.first()
-    bands(0, lf_ref)
-
-    copy(tok_ref, tprev, tok_s, tok_r, mate).wait_recv()
-    for tile in range(2):
-        row = tprev[tile + 6 : tile + 7, :]
-        row = jnp.where(s == 0, -1, row)
-        oneh[:, tile * 128 : (tile + 1) * 128] = jnp.where(ids == row, 1.0, 0.0).astype(BF16)
+
+    @pl.when(x != y)
+    def _():
+        copy(wosend, wt.at[zc, x], wo_s, wo_r, mate).wait()
+
+    outw.xsend()
 
     pair0 = z // 2
     even = 1 - 2 * lax.rem(z, 2)
@@ -242,7 +288,7 @@
     lane = lax.broadcasted_iota(jnp.int32, (16, 128), 1)
 
     def fir(rows, tap, first):
-        f = [jnp.broadcast_to(tap[:, n : n + 1], (16, 128)) for n in range(7)]
+        f = [jnp.broadcast_to(tap[:, n : n + 1], (16, 128)).astype(BF16) for n in range(7)]
         outs = {}
         for tile in range(first - 1, TILES):
             cur = proj[pl.ds(rows, 16), tile * 128 : (tile + 1) * 128]
@@ -268,7 +314,7 @@
         for n in range(5):
             proj[:, n * 256 : (n + 1) * 256] = jnp.dot(
                 left, oneh[:, n * 256 : (n + 1) * 256], preferred_element_type=F32
-            )
+            ).astype(BF16)
 
         def group(g, carry):
             ch = pl.multiple_of(g * 16, 16)
@@ -276,18 +322,16 @@
             tap = [taps[which, p, part, pl.ds(ch, 16), :] for part in range(3)]
             key = fir(pl.multiple_of(base + 32, 16), tap[1], 1)
             val = fir(pl.multiple_of(base + 64, 16), tap[2], 1)
-            prod = {tile: (key[tile] * val[tile]).astype(BF16) for tile in key}
+            prod = {tile: key[tile] * val[tile] for tile in key}
             rows = jnp.concatenate(
                 [jnp.concatenate([prod[t - 1], prod[t]], axis=1) for t in range(2, TILES)], axis=0
             )
-            conv = jnp.dot(rows, band[which, 8 * p + g], preferred_element_type=F32)
+            conv = jnp.dot(rows, band[which, 8 * p + g], preferred_element_type=F32).astype(BF16)
             query = fir(pl.multiple_of(base, 16), tap[0], 2)
-            skip = jnp.broadcast_to(tap[0][:, 7:8], (16, 128))
+            skip = jnp.broadcast_to(tap[0][:, 7:8], (16, 128)).astype(BF16)
             for t in range(2, TILES):
-                whole = conv[(t - 2) * 16 : (t - 1) * 16] + skip * prod[t].astype(F32)
-                g4[k, p, pl.ds(ch, 16), (t - 2) * 128 : (t - 1) * 128] = (
-                    query[t] * whole
-                ).astype(BF16)
+                whole = conv[(t - 2) * 16 : (t - 1) * 16] + skip * prod[t]
+                g4[k, p, pl.ds(ch, 16), (t - 2) * 128 : (t - 1) * 128] = query[t] * whole
             return carry
 
         lax.fori_loop(0, 8, group, 0)
@@ -314,37 +358,28 @@
         block(1, far, pair(i))
 
     table_own.step(1)
+    copy(tt.at[0, zc, x], tt.at[1, zc, x], t2_s, t2_r, mate).wait_recv()
+    table_far.xsend()
     own(1)
     table_own.step(2)
-    copy(tt.at[0, zc, x], tt.at[1, zc, x], t2_s, t2_r, mate).wait_recv()
     table_far.first()
     own(2)
     table_own.step(3)
     table_far.step(1)
-
-    @pl.when(x != y)
-    def _():
-        copy(wo_ref, wt.at[zc, x], wo_s, wo_r, mate).wait()
-
-    outw.first()
     own(3)
     table_own.step(4)
     table_far.step(2)
-    outw.step(1)
+    outw.first()
     own(4)
     table_far.step(3)
-    outw.step(2)
-    for n in range(2):
-        ref = (sf2, lf2)[n]
-        copy(ref, ref, fil_s.at[n], fil_r.at[n], mate).wait_recv()
-    columns(1, sf2)
-    bands(1, lf2)
+    outw.step(1)
     others(1)
     table_far.step(4)
+    outw.step(2)
+    others(2)
     outw.step(3)
-    others(2)
+    others(3)
     outw.step(4)
-    others(3)
     others(4)
     for i in range(1, 5):
         outw.settle(i)
@@ -371,15 +406,22 @@
     for i in range(1, 5):
         gwait(i)
 
+    def written(n):
+        rows = pl.ds(pl.multiple_of(n * 128, 128), 128)
+        return pltpu.make_async_copy(stage.at[rows], out_ref.at[rows], out_s.at[n])
+
     def rest(n, carry):
         rows = pl.ds(pl.multiple_of(n * 128, 128), 128)
         ks = (lax.rem(y + 1, NY), lax.rem(y + 3, NY))
-        out_ref[rows, :] = (acc[rows, :] + project(ks, n)).astype(BF16)
+        stage[rows, :] = (acc[rows, :] + project(ks, n)).astype(BF16)
+        written(n).start()
         return carry
 
     lax.fori_loop(0, 4, rest, 0)
     for one in sent:
         one.wait_send()
+    for n in range(4):
+        written(n).wait()
 
 
 def body(
@@ -387,24 +429,22 @@
 ):
     tok = token_ids.reshape(8, 128)
     gain = norm_gain.reshape(4, 1, 512)
-    w = in_weight.reshape(32, 3, 16, 32).transpose(2, 0, 1, 3).reshape(16, 32, 96)
-    w = jnp.pad(w, ((0, 0), (0, 0), (0, 32)))
-    wo = out_weight.T.reshape(32, 4, 128).transpose(1, 0, 2)
-    skip = jnp.broadcast_to(long_skip[None, None, :], (1, 3, 512))
-    sf = jnp.concatenate([short_filter, skip], axis=0)
-    sf = sf.reshape(8, 3, 4, 128).transpose(2, 1, 0, 3)
-    lf = long_filter.astype(F32)
+    w = in_weight.transpose(1, 0, 2)
+    short = short_filter.transpose(1, 0, 2)
+    skip = long_skip.reshape(1, 512)
     vmem = pl.BlockSpec(memory_space=pltpu.VMEM)
     dma = pltpu.SemaphoreType.DMA
     out = pl.pallas_call(
         kernel,
         out_shape=jax.ShapeDtypeStruct((512, 1024), BF16),
-        in_specs=[vmem] * 7,
-        out_specs=vmem,
+        in_specs=[vmem] * 8,
+        out_specs=pl.BlockSpec(memory_space=pl.ANY),
         scratch_shapes=[
             pltpu.VMEM((8, 128), jnp.int32),
-            pltpu.VMEM((4, 3, 8, 128), F32),
-            pltpu.VMEM((32, 128), F32),
+            pltpu.VMEM((2, 4, 3, 8, 128), F32),
+            pltpu.VMEM((2, 32, 128), F32),
+            pltpu.VMEM((LINE, 32, 128), BF16),
+            pltpu.VMEM((4, 32, 128), BF16),
             pltpu.VMEM((NX, LINE, 32, 128), BF16),
             pltpu.VMEM((NY, 128, 512), BF16),
             pltpu.VMEM((2, LINE, NX, 96, 128), BF16),
@@ -413,17 +453,18 @@
             pltpu.VMEM((512, TILES * 128), BF16),
             pltpu.VMEM((2, 32, 256, 128), BF16),
             pltpu.VMEM((2, 4, 3, 128, 8), F32),
-            pltpu.VMEM((384, TILES * 128), F32),
+            pltpu.VMEM((384, TILES * 128), BF16),
             pltpu.VMEM((512, 1024), F32),
+            pltpu.VMEM((512, 1024), BF16),
             dma, dma, dma((2,)), dma((2,)), dma((LINE - 1,)), dma((LINE - 1,)),
-            dma((3,)), dma((3,)), dma((3,)), dma((3,)), dma, dma, dma, dma,
+            dma((3, 2)), dma((3, 2)), dma((2, 3)), dma((2, 3)), dma, dma, dma, dma,
             dma((3, 3)), dma((3, 3)), dma((3, 2, 4, 4)), dma((3, 2, 4, 4)),
-            dma((3, 8)), dma((3, 8)), dma((2, 4)), dma((2, 4)),
+            dma((3, 8)), dma((3, 8)), dma((2, 4)), dma((2, 4)), dma((4,)),
         ],
         compiler_params=pltpu.CompilerParams(
             collective_id=0, has_side_effects=True, vmem_limit_bytes=60 * 2**20
         ),
-    )(tok, embed_table, gain, w, wo, sf, lf)
+    )(tok, embed_table, gain, w, out_weight.T, short, skip, long_filter)
     return out.T
 
 

time: 107 us -> 79.1 us (0.74)
  Pallas kernels: 101 us -> 76.4 us
  local copies, waits for them, and re-layouts: 5.07 us -> 2.28 us
  other arithmetic: 1.22 us -> 0 us
    pallas_call x1, Pallas kernels: 101 us -> 76.4 us  [body(): pl.pallas_call(kernel, out_shape=jax.ShapeDtypeStruct((512, 1024), BF16),...]
where the time goes in v2:
time: 79.1 us; the launch traced here: 78.7 us
  Pallas kernels  76.4 us (97%)
  local copies, waits for them, and re-layouts  2.28 us (3%)
    pallas_call x1, Pallas kernels, body(): pl.pallas_call(kernel, out_shape=jax.ShapeDtypeStruct((512, 1024), BF16),...  76.4 us
    transpose x1, local copies, waits for them, and re-layouts, body(): return out.T  2.28 us

profile of v2, /device:TPU:1, one launch (start us, length us, event | category | flops | bytes accessed | tf_op | source)
XLA Modules:
  0.0 78.7 jit_solution(3909139844802402980)
XLA Ops:
  0.0 76.4 %shard_map.82 = bf16[512,1024]{1,0:T(8,128)(2,1)} custom-call(s32[8,128]{1,0:T(8,128)} %bitcast.12, bf16[512,512]{1,0:T(8,128)(2,1)} %emb_ref.1, f32[4,1,512]{2,1,0:T(1,128)} %bitcast.11, bf16[3,32,512]{2,1,0:T(8,128)(2,1)} %bitcast.8, bf16[32,512]{1,0:T(8,128)(2,1)} %bitcast.10, f32[3,7,512]{2,1,0:T(8,128)} %bitcast.9, f32[1,512]{1,0:T(1,128)} %bitcast.13, ...), custom_call_target="tpu_custom_call" | custom-call | tf_op jit(solution)/shard_map/pallas_call | solution.py:437
  76.4 2.3 %copy.9 = bf16[1024,512]{1,0:T(8,128)(2,1)} copy(bf16[1024,512]{0,1:T(8,128)(2,1)} %bitcast.7) | data formatting | bytes 2097152 | tf_op jit(solution)/shard_map/transpose | solution.py:468

commit v3 on v2

v3 whole, which is shorter than its diff:
```python
import functools

import jax
import jax.numpy as jnp
from jax import lax
from jax.experimental import pallas as pl
from jax.experimental.pallas import tpu as pltpu
from jax.sharding import PartitionSpec as P

MESH = pl.DeviceIdType.MESH
BF16 = jnp.bfloat16
F32 = jnp.float32
NX, NZ, NC, NY = 4, 8, 2, 4
LINE = NZ * NC
TILES = 10


def kernel(
    tok_ref, emb_ref, gain_ref, w_ref, wo_ref, short_ref, skip_ref, long_ref, out_ref,
    tprev, sf, lf, wsend, wosend, wl, e4, tt, wt, g4, oneh, band, taps, tabn, proj, pt, qt, acc, stage,
    tok_s, tok_r, fil_s, fil_r, s1_s, s1_r, s2_s, s2_r, e_s, e_r, wo_s, wo_r, t2_s, t2_r,
    ax_s, ax_r, az_s, az_r, ad_s, ad_r, g_s, g_r, out_s,
):
    s = lax.axis_index("seq")
    y = lax.axis_index("tp")
    zc = lax.rem(s, LINE)
    x = s // LINE
    z = zc // NC
    c = lax.rem(zc, NC)
    sign = 1 - 2 * c
    far = lax.rem(y + 2, NY)
    turned = y * LINE + zc

    def at_x(q):
        return (lax.rem(x + q, NX) * LINE + zc, y)

    def at_y(q):
        return (s, lax.rem(y + q, NY))

    def at_z(q):
        return (x * LINE + lax.rem(z + q + NZ, NZ) * NC + c, y)

    mate = (s + sign, y)
    after = (lax.rem(s + 1, NX * LINE), y)
    before = (lax.rem(s + NX * LINE - 1, NX * LINE), y)

    def copy(src, dst, ss, rs, dev):
        return pltpu.make_async_remote_copy(
            src_ref=src, dst_ref=dst, send_sem=ss, recv_sem=rs, device_id=dev, device_id_type=MESH
        )

    def send(*args):
        copy(*args).start()

    def got(ref, rs):
        copy(ref, ref, tok_s, rs, mate).wait_recv()

    def gone(ref, ss):
        copy(ref, ref, ss, tok_r, mate).wait_send()

    hello = pltpu.get_barrier_semaphore()
    greeted = 0
    for r in range(1, LINE):
        pl.semaphore_signal(
            hello, inc=1, device_id=(x * LINE + lax.rem(zc + r, LINE), y), device_id_type=MESH
        )
        greeted += 1
    for r in range(1, NX):
        pl.semaphore_signal(hello, inc=1, device_id=at_x(r), device_id_type=MESH)
        pl.semaphore_signal(hello, inc=1, device_id=at_y(r), device_id_type=MESH)
        greeted += 2
    pl.semaphore_signal(hello, inc=1, device_id=after, device_id_type=MESH)
    pl.semaphore_signal(hello, inc=1, device_id=before, device_id_type=MESH)
    greeted += 2

    @pl.when(x != y)
    def _():
        pl.semaphore_signal(hello, inc=1, device_id=(turned, x), device_id_type=MESH)

    lane32 = lax.broadcasted_iota(jnp.int32, (32, 128), 1) // 32
    for p in range(4):
        chunk = [w_ref[part, :, p * 128 : (p + 1) * 128] for part in range(3)]
        for n in range(4):
            moved = [
                chunk[part] if part == n else pltpu.roll(chunk[part], (part - n) % 4 * 32, 1)
                for part in range(3)
            ]
            wsend[4 * p + n] = jnp.where(
                lane32 == 0, moved[0], jnp.where(lane32 == 1, moved[1], moved[2])
            )
        wosend[p] = wo_ref[:, p * 128 : (p + 1) * 128]
        for part in range(3):
            sf[0, p, part, 0:7, :] = short_ref[part, :, p * 128 : (p + 1) * 128]
            sf[0, p, part, 7:8, :] = skip_ref[:, p * 128 : (p + 1) * 128]
    lf[0] = long_ref[...].astype(F32)
    wl[x, zc] = wsend[zc]
    e4[y] = emb_ref[pl.ds(pl.multiple_of(x * 128, 128), 128), :]

    @pl.when(x == y)
    def _():
        wt[zc, x] = wosend[...]

    ids = lax.broadcasted_iota(jnp.int32, (128, 512), 1)

    def onehot(tile, column):
        oneh[tile * 128 : (tile + 1) * 128, :] = jnp.where(
            ids == jnp.broadcast_to(column, (128, 512)), 1.0, 0.0
        ).astype(BF16)

    names = tok_ref[...].T
    for tile in range(8):
        onehot(tile + 2, names[:, tile : tile + 1])

    above = lax.broadcasted_iota(jnp.int32, (128, 128), 1) >= lax.broadcasted_iota(
        jnp.int32, (128, 128), 0
    )

    def bands(which, begin, end):
        def build(g, carry):
            rows = jnp.broadcast_to(lf[which, pl.ds(g, 1), :], (128, 128))
            moved = pltpu.roll(rows, 0, 1, stride=1, stride_axis=0)
            band[which, g, 0:128, :] = jnp.where(above, 0.0, moved).astype(BF16)
            band[which, g, 128:256, :] = jnp.where(above, moved, 0.0).astype(BF16)
            return carry

        lax.fori_loop(begin, end, build, 0)

    def columns(which):
        for p in range(4):
            taps[which, p] = sf[which, p, 0].T

    columns(0)
    bands(0, 0, 32)
    pl.semaphore_wait(hello, greeted + jnp.where(x == y, 0, 1))

    half = pl.ds(pl.multiple_of(64 * c, 64), 64)
    other = pl.ds(pl.multiple_of(64 - 64 * c, 64), 64)
    for r in (8, 7, 9, 6, 10, 5, 11, 4, 12, 3, 13, 2, 14, 1, 15):
        to = lax.rem(zc + r, LINE)
        send(wsend.at[to], wl.at[x, zc], s1_s, s1_r, (x * LINE + to, y))
    for r in (2, 1, 3):
        send(
            emb_ref.at[pl.ds(pl.multiple_of(x * 128 + 64 * c, 64), 64)],
            e4.at[y, half], e_s.at[0], e_r.at[r - 1], at_y(r),
        )
    send(tok_ref, tprev, tok_s, tok_r, after)
    send(sf.at[0], sf.at[1], fil_s.at[0], fil_r.at[0], at_y(2))
    send(lf.at[0], lf.at[1], fil_s.at[1], fil_r.at[1], at_y(2))

    @pl.when(x != y)
    def _():
        copy(wosend, wt.at[zc, y], wo_s, wo_r, (turned, x)).start()

    got(wl.at[x, pl.ds(0, LINE - 1)], s1_r)

    parts = (pl.ds(0, 8), pl.ds(8, 8))
    for way, q in ((0, 1), (1, 3)):
        for n in (way, 1 - way):
            here = wl.at[x, parts[n]]
            send(here, here, s2_s, s2_r.at[way, n], at_x(q))
    for r in (1, 3, 2):
        here = e4.at[lax.rem(y + NY - r, NY), half]
        got(here, e_r.at[r - 1])
        send(here, here, e_s.at[1], e_r.at[3], mate)
    for way, q in ((0, 1), (1, 3)):
        here = wl.at[lax.rem(x + NX - q, NX), parts[way]]
        got(here, s2_r.at[way, way])
        send(here, here, s2_s, s2_r.at[2, way], at_x(q))
    got(e4.at[pl.ds(0, 3), other], e_r.at[3])

    total = jnp.zeros((128, 1), F32)
    for k in range(NY):
        piece = e4[k].astype(F32)
        total = total + jnp.sum(piece * piece, axis=1, keepdims=True)
    scale = lax.rsqrt(total * (1.0 / 2048) + 1e-06)
    normed = [
        (e4[k].astype(F32) * scale * gain_ref[k]).astype(BF16) for k in range(NY)
    ]
    got(tprev, tok_r)
    names = jnp.where(s == 0, -1, tprev[...]).T
    for tile in range(2):
        onehot(tile, names[:, tile + 6 : tile + 7])

    for way, q in ((0, 1), (1, 3)):
        here = wl.at[lax.rem(x + NX - q, NX), parts[1 - way]]
        got(here, s2_r.at[way, 1 - way])
    for way in range(2):
        here = wl.at[lax.rem(x + 2, NX), parts[way]]
        got(here, s2_r.at[2, way])
    table = jnp.zeros((128, 128), F32)
    for k in range(NX):
        table = table + jnp.dot(
            normed[k], wl[k].reshape(512, 128), preferred_element_type=F32
        )
    tt[0, zc, x] = table.T[0:96].astype(BF16)

    class Gather:
        def __init__(self, n, buf):
            self.n, self.buf = n, buf
            self.fine = n == 0
            self.units = range(NX) if self.fine else (None,)

        def ref(self, block, unit):
            if unit is None:
                return self.buf.at[block]
            return self.buf.at[block, lax.rem(x + NX - unit, NX)]

        def arrived(self, way, step, unit):
            if self.fine:
                return az_r.at[(way * 4 + step - 1) * 4 + unit]
            return az_r.at[24 + self.n * 8 + way * 4 + step - 1]

        def xsend(self):
            here = self.buf.at[zc, x]
            for q in range(1, NX):
                send(here, here, ax_s.at[self.n], ax_r.at[q - 1 if self.fine else 2 + self.n], at_x(q))

        def zsend(self, way, step, unit):
            hop = sign if way == 0 else -sign
            here = self.ref(lax.rem(z - hop * (step - 1) + NZ, NZ) * NC + c, unit)
            send(here, here, az_s.at[self.n], self.arrived(way, step, unit), at_z(hop))

        def zwait(self, way, step, unit):
            hop = sign if way == 0 else -sign
            block = lax.rem(z - hop * step + NZ, NZ) * NC + c
            got(self.ref(block, unit), self.arrived(way, step, unit))
            return block

        def dsend(self, step, block):
            here = self.buf.at[block]
            send(here, here, ad_s.at[self.n], ad_r.at[self.n, step - 1], mate)

        def first(self):
            if not self.fine:
                got(self.buf.at[zc, pl.ds(0, 3)], ax_r.at[2 + self.n])
            for unit in self.units:
                if unit:
                    got(self.ref(zc, unit), ax_r.at[unit - 1])
                self.zsend(0, 1, unit)
                self.zsend(1, 1, unit)
            self.dsend(1, zc)

        def step(self, i):
            blocks = []
            for unit in self.units:
                for way in range(2):
                    last = 4 if way == 0 else 3
                    if i <= last:
                        block = self.zwait(way, i, unit)
                        if not unit:
                            blocks.append(block)
                        if i < last:
                            self.zsend(way, i + 1, unit)
            for block in blocks:
                self.dsend(i, block)

        def settle(self, i):
            got(self.buf.at[pl.ds(0, (3, 2, 2, 1)[i - 1])], ad_r.at[self.n, i - 1])

        def close(self):
            gone(self.buf.at[0, pl.ds(0, 3)], ax_s.at[self.n])
            gone(self.buf.at[pl.ds(0, 7)], az_s.at[self.n])
            gone(self.buf.at[pl.ds(0, 8)], ad_s.at[self.n])

    table_own = Gather(0, tt.at[0])
    table_far = Gather(1, tt.at[1])
    outw = Gather(2, wt)

    table_own.xsend()
    send(tt.at[0, zc, x], tt.at[1, zc, x], t2_s, t2_r, at_y(2))
    got(sf.at[1], fil_r.at[0])
    got(lf.at[1], fil_r.at[1])
    columns(1)
    bands(1, 0, 16)
    table_own.first()

    @pl.when(x != y)
    def _():
        copy(wosend, wt.at[zc, x], wo_s, wo_r, mate).wait()

    outw.xsend()
    bands(1, 16, 32)

    pair0 = z // 2
    even = 1 - 2 * lax.rem(z, 2)

    def pair(i):
        move = (0, -even, even, 2)[i - 1]
        return lax.rem(pair0 + move + 4, 4)

    def block(which, k, p):
        table = jnp.concatenate(
            [
                jnp.concatenate(
                    [
                        tt[which, 4 * p + n, b, part * 32 : (part + 1) * 32, :]
                        for part in range(3)
                        for n in range(4)
                    ],
                    axis=0,
                )
                for b in range(NX)
            ],
            axis=1,
        )
        tabn[...] = table.T
        for n in range(5):
            rows = slice(n * 256, (n + 1) * 256)
            both = jnp.dot(oneh[rows, :], tabn[...], preferred_element_type=F32)
            for part in range(3):
                proj[part, rows, :] = both[:, part * 128 : (part + 1) * 128]

        def fir(part, row, count):
            total = None
            for lag in range(7):
                tap = jnp.broadcast_to(sf[which, p, part, lag : lag + 1, :], (count, 128))
                term = tap * proj[part, pl.ds(row - lag, count), :]
                total = term if total is None else total + term
            return total

        def tile(n, carry):
            row = pl.multiple_of(n * 128, 128)
            prod, query = [], []
            for h in range(4):
                prod.append((fir(1, row + 32 * h, 32) * fir(2, row + 32 * h, 32)).astype(BF16))
                query.append(fir(0, row + 32 * h, 32).astype(BF16))
            pt[n] = jnp.concatenate(prod, axis=0).T
            qt[n] = jnp.concatenate(query, axis=0).T
            return carry

        lax.fori_loop(1, TILES, tile, 0)

        def groups(h, carry):
            for n in range(4):
                g = 4 * h + n
                ch = pl.ds(pl.multiple_of(g * 16, 16), 16)
                prod = [pt[t, ch, :] for t in range(1, TILES)]
                rows = jnp.concatenate(
                    [jnp.concatenate([prod[t], prod[t + 1]], axis=1) for t in range(8)], axis=0
                )
                conv = jnp.dot(rows, band[which, 8 * p + g], preferred_element_type=F32).astype(BF16)
                skip = jnp.broadcast_to(taps[which, p, ch, 7:8], (16, 128)).astype(BF16)
                for t in range(8):
                    whole = conv[t * 16 : (t + 1) * 16] + skip * prod[t + 1]
                    g4[k, p, ch, t * 128 : (t + 1) * 128] = qt[t + 2, ch, :] * whole
            return carry

        lax.fori_loop(0, 2, groups, 0)

    def gsend(i):
        here = g4.at[y, pair(i)]
        for way, q in ((0, 1), (1, 3)):
            send(here, here, g_s, g_r.at[way], at_y(q))

    def own(i):
        table_own.settle(i)
        block(0, y, pair(i))
        gsend(i)

    def others(i):
        table_far.settle(i)
        block(1, far, pair(i))

    table_own.step(1)
    got(tt.at[1, zc, x], t2_r)
    table_far.xsend()
    own(1)
    table_own.step(2)
    table_far.first()
    own(2)
    table_own.step(3)
    table_far.step(1)
    own(3)
    table_own.step(4)
    table_far.step(2)
    outw.first()
    own(4)
    table_far.step(3)
    outw.step(1)
    others(1)
    table_far.step(4)
    outw.step(2)
    others(2)
    outw.step(3)
    others(3)
    outw.step(4)
    others(4)
    for i in range(1, 5):
        outw.settle(i)

    def project(ks, n):
        sums = None
        for k in ks:
            left = jnp.concatenate(
                [wt[pl.ds(4 * n, 4), k, p].reshape(128, 128) for p in range(4)], axis=1
            )
            term = jnp.dot(left, g4[k].reshape(512, 1024), preferred_element_type=F32)
            sums = term if sums is None else sums + term
        return sums

    def near(n, carry):
        cols = pl.ds(pl.multiple_of(n * 128, 128), 128)
        resid = lax.dot_general(
            emb_ref[:, cols], oneh[256:, :], (((0,), (1,)), ((), ())), preferred_element_type=F32
        )
        acc[cols, :] = resid + project((y, far), n)
        return carry

    lax.fori_loop(0, 4, near, 0)
    for way, q in ((0, 3), (1, 1)):
        got(g4.at[lax.rem(y + q, NY)], g_r.at[way])

    def rest(n, carry):
        rows = pl.ds(pl.multiple_of(n * 128, 128), 128)
        ks = (lax.rem(y + 1, NY), lax.rem(y + 3, NY))
        stage[rows, :] = (acc[rows, :] + project(ks, n)).astype(BF16)
        pltpu.make_async_copy(stage.at[rows], out_ref.at[rows], out_s).start()
        return carry

    lax.fori_loop(0, 4, rest, 0)
    gone(wsend.at[pl.ds(0, LINE - 1)], s1_s)
    gone(wl.at[pl.ds(0, 3)], s2_s)
    for n in range(2):
        gone(e4.at[pl.ds(0, 3), half], e_s.at[n])
        gone((sf, lf)[n].at[0], fil_s.at[n])
    gone(tok_ref, tok_s)
    gone(tt.at[0, zc, x], t2_s)
    gone(g4.at[pl.ds(0, 2)], g_s)
    for one in (table_own, table_far, outw):
        one.close()
    pltpu.make_async_copy(stage, out_ref, out_s).wait()


def body(
    token_ids, embed_table, norm_gain, in_weight, short_filter, long_filter, long_skip, out_weight
):
    tok = token_ids.reshape(8, 128)
    gain = norm_gain.reshape(4, 1, 512)
    w = in_weight.transpose(1, 0, 2)
    short = short_filter.transpose(1, 0, 2)
    skip = long_skip.reshape(1, 512)
    vmem = pl.BlockSpec(memory_space=pltpu.VMEM)
    dma = pltpu.SemaphoreType.DMA
    out = pl.pallas_call(
        kernel,
        out_shape=jax.ShapeDtypeStruct((512, 1024), BF16),
        in_specs=[vmem] * 8,
        out_specs=pl.BlockSpec(memory_space=pl.ANY),
        scratch_shapes=[
            pltpu.VMEM((8, 128), jnp.int32),
            pltpu.VMEM((2, 4, 3, 8, 128), F32),
            pltpu.VMEM((2, 32, 128), F32),
            pltpu.VMEM((LINE, 32, 128), BF16),
            pltpu.VMEM((4, 32, 128), BF16),
            pltpu.VMEM((NX, LINE, 32, 128), BF16),
            pltpu.VMEM((NY, 128, 512), BF16),
            pltpu.VMEM((2, LINE, NX, 96, 128), BF16),
            pltpu.VMEM((LINE, NX, 4, 32, 128), BF16),
            pltpu.VMEM((NY, 4, 128, 1024), BF16),
            pltpu.VMEM((TILES * 128, 512), BF16),
            pltpu.VMEM((2, 32, 256, 128), BF16),
            pltpu.VMEM((2, 4, 128, 8), F32),
            pltpu.VMEM((512, 384), BF16),
            pltpu.VMEM((3, TILES * 128, 128), F32),
            pltpu.VMEM((TILES, 128, 128), BF16),
            pltpu.VMEM((TILES, 128, 128), BF16),
            pltpu.VMEM((512, 1024), F32),
            pltpu.VMEM((512, 1024), BF16),
            dma, dma, dma((2,)), dma((2,)), dma, dma, dma, dma((3, 2)),
            dma((2,)), dma((4,)), dma, dma, dma, dma,
            dma((3,)), dma((5,)), dma((3,)), dma((48,)), dma((3,)), dma((3, 4)), dma, dma((2,)), dma,
        ],
        compiler_params=pltpu.CompilerParams(
            collective_id=0, has_side_effects=True, vmem_limit_bytes=60 * 2**20
        ),
    )(tok, embed_table, gain, w, out_weight.T, short, skip, long_filter)
    return out.T


def solution(mesh):
    placed = (
        P("seq"),
        P(None, "tp"),
        P(),
        P("seq", None, "tp"),
        P(None, None, "tp"),
        P("tp", None),
        P("tp"),
        P("tp", "seq"),
    )
    return jax.shard_map(
        body, mesh=mesh, in_specs=placed, out_specs=P("seq", "tp"), check_vma=False
    )
```

time: 79.1 us -> 78 us (0.986)
  Pallas kernels: 76.4 us -> 75.2 us
    pallas_call x1, Pallas kernels: 76.4 us -> 75.2 us  [body(): pl.pallas_call(kernel, out_shape=jax.ShapeDtypeStruct((512, 1024), BF16),...]
where the time goes in v3:
time: 78 us; the launch traced here: 77.5 us
  Pallas kernels  75.2 us (96%)
  local copies, waits for them, and re-layouts  2.28 us (3%)
    pallas_call x1, Pallas kernels, body(): pl.pallas_call(kernel, out_shape=jax.ShapeDtypeStruct((512, 1024), BF16),...  75.2 us
    transpose x1, local copies, waits for them, and re-layouts, body(): return out.T  2.28 us

profile of v3, /device:TPU:1, one launch (start us, length us, event | category | flops | bytes accessed | tf_op | source)
XLA Modules:
  0.0 77.5 jit_solution(2033301753569458462)
XLA Ops:
  0.0 75.2 %shard_map.82 = bf16[512,1024]{1,0:T(8,128)(2,1)} custom-call(s32[8,128]{1,0:T(8,128)} %bitcast.12, bf16[512,512]{1,0:T(8,128)(2,1)} %emb_ref.1, f32[4,1,512]{2,1,0:T(1,128)} %bitcast.11, bf16[3,32,512]{2,1,0:T(8,128)(2,1)} %bitcast.8, bf16[32,512]{1,0:T(8,128)(2,1)} %bitcast.10, f32[3,7,512]{2,1,0:T(8,128)} %bitcast.9, f32[1,512]{1,0:T(1,128)} %bitcast.13, ...), custom_call_target="tpu_custom_call" | custom-call | tf_op jit(solution)/shard_map/pallas_call | solution.py:444
  75.2 2.3 %copy.9 = bf16[1024,512]{1,0:T(8,128)(2,1)} copy(bf16[1024,512]{0,1:T(8,128)(2,1)} %bitcast.7) | data formatting | bytes 2097152 | tf_op jit(solution)/shard_map/transpose | solution.py:477

commit v4 on v3

--- a/solution.py
+++ b/solution.py
@@ -17,9 +17,9 @@
 
 def kernel(
     tok_ref, emb_ref, gain_ref, w_ref, wo_ref, short_ref, skip_ref, long_ref, out_ref,
-    tprev, sf, lf, wsend, wosend, wl, e4, tt, wt, g4, oneh, band, taps, tabn, proj, pt, qt, acc, stage,
-    tok_s, tok_r, fil_s, fil_r, s1_s, s1_r, s2_s, s2_r, e_s, e_r, wo_s, wo_r, t2_s, t2_r,
-    ax_s, ax_r, az_s, az_r, ad_s, ad_r, g_s, g_r, out_s,
+    tprev, sf, lf, wsend, wosend, wl, e4, tt, wt, g4, oneh, band, taps, tabn, proj, pt, qt, onet, acc, stage,
+    tok_s, tok_r, fil_s, fil_r, s1_s, s1_r, s2_s, s2_r, far_r, e_s, e_r, wo_s, wo_r, t2_s, t2_r,
+    ax_s, ax_r, az_s, az_r, ad_s, ad_r, wz_s, wz_r, wx_s, wx_r, wd_s, wd_r, tx_r, td_r, g_s, g_r, out_s,
 ):
     s = lax.axis_index("seq")
     y = lax.axis_index("tp")
@@ -98,46 +98,18 @@
 
     @pl.when(x == y)
     def _():
-        wt[zc, x] = wosend[...]
-
-    ids = lax.broadcasted_iota(jnp.int32, (128, 512), 1)
-
-    def onehot(tile, column):
-        oneh[tile * 128 : (tile + 1) * 128, :] = jnp.where(
-            ids == jnp.broadcast_to(column, (128, 512)), 1.0, 0.0
-        ).astype(BF16)
-
-    names = tok_ref[...].T
-    for tile in range(8):
-        onehot(tile + 2, names[:, tile : tile + 1])
-
-    above = lax.broadcasted_iota(jnp.int32, (128, 128), 1) >= lax.broadcasted_iota(
-        jnp.int32, (128, 128), 0
-    )
-
-    def bands(which, begin, end):
-        def build(g, carry):
-            rows = jnp.broadcast_to(lf[which, pl.ds(g, 1), :], (128, 128))
-            moved = pltpu.roll(rows, 0, 1, stride=1, stride_axis=0)
-            band[which, g, 0:128, :] = jnp.where(above, 0.0, moved).astype(BF16)
-            band[which, g, 128:256, :] = jnp.where(above, moved, 0.0).astype(BF16)
-            return carry
-
-        lax.fori_loop(begin, end, build, 0)
-
-    def columns(which):
-        for p in range(4):
-            taps[which, p] = sf[which, p, 0].T
-
-    columns(0)
-    bands(0, 0, 32)
+        wt[z, c, x] = wosend[...]
+
     pl.semaphore_wait(hello, greeted + jnp.where(x == y, 0, 1))
 
     half = pl.ds(pl.multiple_of(64 * c, 64), 64)
     other = pl.ds(pl.multiple_of(64 - 64 * c, 64), 64)
-    for r in (8, 7, 9, 6, 10, 5, 11, 4, 12, 3, 13, 2, 14, 1, 15):
-        to = lax.rem(zc + r, LINE)
-        send(wsend.at[to], wl.at[x, zc], s1_s, s1_r, (x * LINE + to, y))
+    order = (4, 3, 5, 2, 6, 1, 7, 0)
+    for d in order:
+        for n in range(NC):
+            if d or n:
+                to = lax.rem(z + d, NZ) * NC + lax.rem(c + n, NC)
+                send(wsend.at[to], wl.at[x, zc], s1_s, s1_r.at[d], (x * LINE + to, y))
     for r in (2, 1, 3):
         send(
             emb_ref.at[pl.ds(pl.multiple_of(x * 128 + 64 * c, 64), 64)],
@@ -149,23 +121,67 @@
 
     @pl.when(x != y)
     def _():
-        copy(wosend, wt.at[zc, y], wo_s, wo_r, (turned, x)).start()
-
-    got(wl.at[x, pl.ds(0, LINE - 1)], s1_r)
-
-    parts = (pl.ds(0, 8), pl.ds(8, 8))
-    for way, q in ((0, 1), (1, 3)):
-        for n in (way, 1 - way):
-            here = wl.at[x, parts[n]]
-            send(here, here, s2_s, s2_r.at[way, n], at_x(q))
+        copy(wosend, wt.at[z, c, y], wo_s, wo_r, (turned, x)).start()
+
+    ids = lax.broadcasted_iota(jnp.int32, (128, 512), 1)
+
+    def onehot(tile, column):
+        oneh[tile * 128 : (tile + 1) * 128, :] = jnp.where(
+            ids == jnp.broadcast_to(column, (128, 512)), 1.0, 0.0
+        ).astype(BF16)
+
+    names = tok_ref[...].T
+    for tile in range(8):
+        onehot(tile + 2, names[:, tile : tile + 1])
+
+    above = lax.broadcasted_iota(jnp.int32, (128, 128), 1) >= lax.broadcasted_iota(
+        jnp.int32, (128, 128), 0
+    )
+
+    def bands(which, begin, end):
+        def build(g, carry):
+            rows = jnp.broadcast_to(lf[which, pl.ds(g, 1), :], (128, 128))
+            moved = pltpu.roll(rows, 0, 1, stride=1, stride_axis=0)
+            band[which, g, 0:128, :] = jnp.where(above, 0.0, moved).astype(BF16)
+            band[which, g, 128:256, :] = jnp.where(above, moved, 0.0).astype(BF16)
+            return carry
+
+        lax.fori_loop(begin, end, build, 0)
+
+    def columns(which):
+        for p in range(4):
+            taps[which, p] = sf[which, p, 0].T
+
+    columns(0)
+    bands(0, 0, 32)
+
+    def unit(q, d):
+        return wl.at[lax.rem(x + q, NX), pl.ds(lax.rem(z + NZ - d, NZ) * NC, NC)]
+
+    def line(d):
+        got(unit(0, d) if d else wl.at[x, pl.ds(zc, 1)], s1_r.at[d])
+        here = unit(0, d)
+        for way, q in ((0, 1), (1, 3)):
+            send(here, here, s2_s, s2_r.at[way, d], at_x(q))
+
+    def relay(k):
+        d = order[-1 - k]
+        for way, q in ((0, 1), (1, 3)):
+            here = unit(NX - q, d)
+            got(here, s2_r.at[way, d])
+            if k % 2 == way:
+                send(here, here, s2_s, far_r.at[way], at_x(q))
+
+    for k in range(NZ):
+        line(order[-1 - k])
+    for k in range(NZ - 2):
+        relay(k)
     for r in (1, 3, 2):
         here = e4.at[lax.rem(y + NY - r, NY), half]
         got(here, e_r.at[r - 1])
         send(here, here, e_s.at[1], e_r.at[3], mate)
-    for way, q in ((0, 1), (1, 3)):
-        here = wl.at[lax.rem(x + NX - q, NX), parts[way]]
-        got(here, s2_r.at[way, way])
-        send(here, here, s2_s, s2_r.at[2, way], at_x(q))
+    relay(NZ - 2)
+    relay(NZ - 1)
     got(e4.at[pl.ds(0, 3), other], e_r.at[3])
 
     total = jnp.zeros((128, 1), F32)
@@ -181,105 +197,126 @@
     for tile in range(2):
         onehot(tile, names[:, tile + 6 : tile + 7])
 
-    for way, q in ((0, 1), (1, 3)):
-        here = wl.at[lax.rem(x + NX - q, NX), parts[1 - way]]
-        got(here, s2_r.at[way, 1 - way])
     for way in range(2):
-        here = wl.at[lax.rem(x + 2, NX), parts[way]]
-        got(here, s2_r.at[2, way])
+        got(wl.at[lax.rem(x + 2, NX), pl.ds(0, 8)], far_r.at[way])
     table = jnp.zeros((128, 128), F32)
     for k in range(NX):
         table = table + jnp.dot(
             normed[k], wl[k].reshape(512, 128), preferred_element_type=F32
         )
-    tt[0, zc, x] = table.T[0:96].astype(BF16)
+    tt[0, z, c, x] = table.T[0:96].astype(BF16)
 
     class Gather:
+        def __init__(self, buf):
+            self.buf = buf
+
+        def ref(self, hop, step):
+            return self.buf.at[lax.rem(z - hop * step + NZ, NZ), c]
+
+        def zsend(self, way, step):
+            hop = sign if way == 0 else -sign
+            here = self.ref(hop, step - 1)
+            send(here, here, az_s, az_r.at[way * 4 + step - 1], at_z(hop))
+
+        def dsend(self, step, here):
+            send(here, here, ad_s, ad_r.at[step - 1], mate)
+
+        def xsend(self):
+            here = self.buf.at[z, c, x]
+            for q in range(1, NX):
+                send(here, here, ax_s, ax_r, at_x(q))
+
+        def first(self):
+            got(self.buf.at[z, c, pl.ds(0, 3)], ax_r)
+            self.zsend(0, 1)
+            self.zsend(1, 1)
+            self.dsend(1, self.ref(0, 0))
+
+        def step(self, i):
+            for way in range(2):
+                last = 4 if way == 0 else 3
+                if i <= last:
+                    here = self.ref(sign if way == 0 else -sign, i)
+                    got(here, az_r.at[way * 4 + i - 1])
+                    if i < last:
+                        self.zsend(way, i + 1)
+                    self.dsend(i, here)
+
+        def settle(self, i):
+            got(self.buf.at[pl.ds(0, (3, 2, 2, 1)[i - 1]), 0], ad_r.at[i - 1])
+
+        def close(self):
+            gone(self.buf.at[0, 0, pl.ds(0, 3)], ax_s)
+            gone(self.buf.at[pl.ds(0, 7), 0], az_s)
+            gone(self.buf.at[:, 0], ad_s)
+
+    class Spread:
         def __init__(self, n, buf):
             self.n, self.buf = n, buf
-            self.fine = n == 0
-            self.units = range(NX) if self.fine else (None,)
-
-        def ref(self, block, unit):
-            if unit is None:
-                return self.buf.at[block]
-            return self.buf.at[block, lax.rem(x + NX - unit, NX)]
-
-        def arrived(self, way, step, unit):
-            if self.fine:
-                return az_r.at[(way * 4 + step - 1) * 4 + unit]
-            return az_r.at[24 + self.n * 8 + way * 4 + step - 1]
-
-        def xsend(self):
-            here = self.buf.at[zc, x]
-            for q in range(1, NX):
-                send(here, here, ax_s.at[self.n], ax_r.at[q - 1 if self.fine else 2 + self.n], at_x(q))
-
-        def zsend(self, way, step, unit):
+
+        def onward(self, way, step):
             hop = sign if way == 0 else -sign
-            here = self.ref(lax.rem(z - hop * (step - 1) + NZ, NZ) * NC + c, unit)
-            send(here, here, az_s.at[self.n], self.arrived(way, step, unit), at_z(hop))
-
-        def zwait(self, way, step, unit):
-            hop = sign if way == 0 else -sign
-            block = lax.rem(z - hop * step + NZ, NZ) * NC + c
-            got(self.ref(block, unit), self.arrived(way, step, unit))
-            return block
-
-        def dsend(self, step, block):
-            here = self.buf.at[block]
-            send(here, here, ad_s.at[self.n], ad_r.at[self.n, step - 1], mate)
-
-        def first(self):
-            if not self.fine:
-                got(self.buf.at[zc, pl.ds(0, 3)], ax_r.at[2 + self.n])
-            for unit in self.units:
-                if unit:
-                    got(self.ref(zc, unit), ax_r.at[unit - 1])
-                self.zsend(0, 1, unit)
-                self.zsend(1, 1, unit)
-            self.dsend(1, zc)
+            here = self.buf.at[lax.rem(z - hop * step + NZ, NZ), c, x]
+            if step:
+                got(here, wz_r.at[self.n, way * 4 + step - 1])
+            if step < (4 if way == 0 else 3):
+                send(here, here, wz_s.at[self.n], wz_r.at[self.n, way * 4 + step], at_z(hop))
+            if step or way == 0:
+                arrive = tx_r.at[step] if self.n == 0 else wx_r
+                for q in (2, 1, 3):
+                    send(here, here, wx_s.at[self.n], arrive, at_x(q))
 
         def step(self, i):
-            blocks = []
-            for unit in self.units:
-                for way in range(2):
-                    last = 4 if way == 0 else 3
-                    if i <= last:
-                        block = self.zwait(way, i, unit)
-                        if not unit:
-                            blocks.append(block)
-                        if i < last:
-                            self.zsend(way, i + 1, unit)
-            for block in blocks:
-                self.dsend(i, block)
+            self.onward(0, i)
+            if i < 4:
+                self.onward(1, i)
+
+        def across(self, i):
+            hops = ((0,), (sign, -sign), (sign, -sign), (sign, -sign), (sign,))[i]
+            got(self.buf.at[pl.ds(0, len(hops)), 0, pl.ds(0, 3)], tx_r.at[i])
+            for hop in hops:
+                here = self.buf.at[lax.rem(z - hop * i + NZ, NZ), c]
+                send(here, here, wd_s.at[0], td_r.at[max(i, 1) - 1], mate)
 
         def settle(self, i):
-            got(self.buf.at[pl.ds(0, (3, 2, 2, 1)[i - 1])], ad_r.at[self.n, i - 1])
+            got(self.buf.at[pl.ds(0, (3, 2, 2, 1)[i - 1]), 0], td_r.at[i - 1])
+
+        def share(self):
+            got(self.buf.at[pl.ds(0, 3)], wx_r)
+            here = self.buf.at[:, c]
+            send(here, here, wd_s.at[1], wd_r, mate)
+
+        def shared(self):
+            got(self.buf.at[:, 1 - c], wd_r)
 
         def close(self):
-            gone(self.buf.at[0, pl.ds(0, 3)], ax_s.at[self.n])
-            gone(self.buf.at[pl.ds(0, 7)], az_s.at[self.n])
-            gone(self.buf.at[pl.ds(0, 8)], ad_s.at[self.n])
-
-    table_own = Gather(0, tt.at[0])
-    table_far = Gather(1, tt.at[1])
-    outw = Gather(2, wt)
-
-    table_own.xsend()
-    send(tt.at[0, zc, x], tt.at[1, zc, x], t2_s, t2_r, at_y(2))
+            gone(self.buf.at[pl.ds(0, 7), 0, 0], wz_s.at[self.n])
+            gone(self.buf.at[pl.ds(0, 3)], wx_s.at[self.n])
+            gone(self.buf.at[:, c], wd_s.at[self.n])
+
+    table_own = Spread(0, tt.at[0])
+    table_far = Gather(tt.at[1])
+    outw = Spread(1, wt)
+
+    table_own.step(0)
+    send(tt.at[0, z, c, x], tt.at[1, z, c, x], t2_s, t2_r, at_y(2))
     got(sf.at[1], fil_r.at[0])
     got(lf.at[1], fil_r.at[1])
     columns(1)
     bands(1, 0, 16)
-    table_own.first()
+    table_own.step(1)
+    bands(1, 16, 24)
+    table_own.step(2)
+    bands(1, 24, 32)
+    got(tt.at[1, z, c, x], t2_r)
+    table_far.xsend()
 
     @pl.when(x != y)
     def _():
-        copy(wosend, wt.at[zc, x], wo_s, wo_r, mate).wait()
-
-    outw.xsend()
-    bands(1, 16, 32)
+        copy(wosend, wt.at[z, c, x], wo_s, wo_r, mate).wait()
+
+    table_own.across(0)
+    table_own.across(1)
 
     pair0 = z // 2
     even = 1 - 2 * lax.rem(z, 2)
@@ -288,12 +325,12 @@
         move = (0, -even, even, 2)[i - 1]
         return lax.rem(pair0 + move + 4, 4)
 
-    def block(which, k, p):
+    def block(which, k, p, early=None, late=None):
         table = jnp.concatenate(
             [
                 jnp.concatenate(
                     [
-                        tt[which, 4 * p + n, b, part * 32 : (part + 1) * 32, :]
+                        tt[which, 2 * p + n // 2, n % 2, b, part * 32 : (part + 1) * 32, :]
                         for part in range(3)
                         for n in range(4)
                     ],
@@ -310,6 +347,9 @@
             for part in range(3):
                 proj[part, rows, :] = both[:, part * 128 : (part + 1) * 128]
 
+        if early:
+            early()
+
         def fir(part, row, count):
             total = None
             for lag in range(7):
@@ -329,6 +369,8 @@
             return carry
 
         lax.fori_loop(1, TILES, tile, 0)
+        if late:
+            late()
 
         def groups(h, carry):
             for n in range(4):
@@ -352,47 +394,67 @@
         for way, q in ((0, 1), (1, 3)):
             send(here, here, g_s, g_r.at[way], at_y(q))
 
-    def own(i):
+    def own(i, **hooks):
         table_own.settle(i)
-        block(0, y, pair(i))
+        block(0, y, pair(i), **hooks)
         gsend(i)
 
-    def others(i):
+    def others(i, **hooks):
         table_far.settle(i)
-        block(1, far, pair(i))
-
-    table_own.step(1)
-    got(tt.at[1, zc, x], t2_r)
-    table_far.xsend()
-    own(1)
-    table_own.step(2)
-    table_far.first()
-    own(2)
-    table_own.step(3)
-    table_far.step(1)
-    own(3)
-    table_own.step(4)
-    table_far.step(2)
-    outw.first()
-    own(4)
-    table_far.step(3)
-    outw.step(1)
-    others(1)
-    table_far.step(4)
-    outw.step(2)
-    others(2)
-    outw.step(3)
+        block(1, far, pair(i), **hooks)
+
+    def resid():
+        below = lax.broadcasted_iota(jnp.int32, (512, 128), 0)
+        for n in range(8):
+            row = tok_ref[n : n + 1, :]
+            onet[:, n * 128 : (n + 1) * 128] = jnp.where(below == row, 1.0, 0.0).astype(BF16)
+        for n in range(4):
+            cols = slice(n * 128, (n + 1) * 128)
+            acc[cols, :] = jnp.dot(emb_ref[:, cols].T, onet[...], preferred_element_type=F32)
+
+    def after1():
+        table_own.step(3)
+        table_own.across(2)
+        table_far.first()
+
+    def after2():
+        table_own.step(4)
+        table_own.across(3)
+        outw.step(0)
+
+    def after3():
+        table_own.across(4)
+        table_far.step(1)
+        outw.step(1)
+
+    def after4():
+        table_far.step(2)
+        outw.step(2)
+
+    def after5():
+        table_far.step(3)
+        outw.step(3)
+
+    def after6():
+        table_far.step(4)
+        outw.step(4)
+
+    own(1, late=after1)
+    resid()
+    own(2, early=after2)
+    own(3, early=after3)
+    own(4, early=after4)
+    others(1, early=after5)
+    others(2, early=after6)
     others(3)
-    outw.step(4)
-    others(4)
-    for i in range(1, 5):
-        outw.settle(i)
+    others(4, early=outw.share)
+    outw.shared()
 
     def project(ks, n):
         sums = None
         for k in ks:
             left = jnp.concatenate(
-                [wt[pl.ds(4 * n, 4), k, p].reshape(128, 128) for p in range(4)], axis=1
+                [wt[pl.ds(2 * n, 2), :, k, p].reshape(128, 128) for p in range(4)], axis=1
             )
             term = jnp.dot(left, g4[k].reshape(512, 1024), preferred_element_type=F32)
             sums = term if sums is None else sums + term
@@ -400,10 +462,7 @@
 
     def near(n, carry):
         cols = pl.ds(pl.multiple_of(n * 128, 128), 128)
-        resid = lax.dot_general(
-            emb_ref[:, cols], oneh[256:, :], (((0,), (1,)), ((), ())), preferred_element_type=F32
-        )
-        acc[cols, :] = resid + project((y, far), n)
+        acc[cols, :] = acc[cols, :] + project((y, far), n)
         return carry
 
     lax.fori_loop(0, 4, near, 0)
@@ -424,7 +483,7 @@
         gone(e4.at[pl.ds(0, 3), half], e_s.at[n])
         gone((sf, lf)[n].at[0], fil_s.at[n])
     gone(tok_ref, tok_s)
-    gone(tt.at[0, zc, x], t2_s)
+    gone(tt.at[0, z, c, x], t2_s)
     gone(g4.at[pl.ds(0, 2)], g_s)
     for one in (table_own, table_far, outw):
         one.close()
@@ -454,8 +513,8 @@
             pltpu.VMEM((4, 32, 128), BF16),
             pltpu.VMEM((NX, LINE, 32, 128), BF16),
             pltpu.VMEM((NY, 128, 512), BF16),
-            pltpu.VMEM((2, LINE, NX, 96, 128), BF16),
-            pltpu.VMEM((LINE, NX, 4, 32, 128), BF16),
+            pltpu.VMEM((2, NZ, NC, NX, 96, 128), BF16),
+            pltpu.VMEM((NZ, NC, NX, 4, 32, 128), BF16),
             pltpu.VMEM((NY, 4, 128, 1024), BF16),
             pltpu.VMEM((TILES * 128, 512), BF16),
             pltpu.VMEM((2, 32, 256, 128), BF16),
@@ -464,11 +523,14 @@
             pltpu.VMEM((3, TILES * 128, 128), F32),
             pltpu.VMEM((TILES, 128, 128), BF16),
             pltpu.VMEM((TILES, 128, 128), BF16),
+            pltpu.VMEM((512, 1024), BF16),
             pltpu.VMEM((512, 1024), F32),
             pltpu.VMEM((512, 1024), BF16),
-            dma, dma, dma((2,)), dma((2,)), dma, dma, dma, dma((3, 2)),
+            dma, dma, dma((2,)), dma((2,)), dma, dma((8,)), dma, dma((2, 8)), dma((2,)),
             dma((2,)), dma((4,)), dma, dma, dma, dma,
-            dma((3,)), dma((5,)), dma((3,)), dma((48,)), dma((3,)), dma((3, 4)), dma, dma((2,)), dma,
+            dma, dma, dma, dma((8,)), dma, dma((4,)),
+            dma((2,)), dma((2, 8)), dma((2,)), dma, dma((2,)), dma, dma((5,)), dma((4,)),
+            dma, dma((2,)), dma,
         ],
         compiler_params=pltpu.CompilerParams(
             collective_id=0, has_side_effects=True, vmem_limit_bytes=60 * 2**20

time: 78 us -> 71.2 us (0.913)
  Pallas kernels: 75.2 us -> 68.8 us
    pallas_call x1, Pallas kernels: 75.2 us -> 68.8 us  [body(): pl.pallas_call(kernel, out_shape=jax.ShapeDtypeStruct((512, 1024), BF16),...]
where the time goes in v4:
time: 71.2 us; the launch traced here: 71.1 us
  Pallas kernels  68.8 us (97%)
  local copies, waits for them, and re-layouts  2.28 us (3%)
    pallas_call x1, Pallas kernels, body(): pl.pallas_call(kernel, out_shape=jax.ShapeDtypeStruct((512, 1024), BF16),...  68.8 us
    transpose x1, local copies, waits for them, and re-layouts, body(): return out.T  2.28 us

profile of v4, /device:TPU:1, one launch (start us, length us, event | category | flops | bytes accessed | tf_op | source)
XLA Modules:
  0.0 71.1 jit_solution(7855785429641291847)
XLA Ops:
  0.0 68.8 %shard_map.82 = bf16[512,1024]{1,0:T(8,128)(2,1)} custom-call(s32[8,128]{1,0:T(8,128)} %bitcast.12, bf16[512,512]{1,0:T(8,128)(2,1)} %emb_ref.1, f32[4,1,512]{2,1,0:T(1,128)} %bitcast.11, bf16[3,32,512]{2,1,0:T(8,128)(2,1)} %bitcast.8, bf16[32,512]{1,0:T(8,128)(2,1)} %bitcast.10, f32[3,7,512]{2,1,0:T(8,128)} %bitcast.9, f32[1,512]{1,0:T(1,128)} %bitcast.13, ...), custom_call_target="tpu_custom_call" | custom-call | tf_op jit(solution)/shard_map/pallas_call | solution.py:503
  68.8 2.3 %copy.9 = bf16[1024,512]{1,0:T(8,128)(2,1)} copy(bf16[1024,512]{0,1:T(8,128)(2,1)} %bitcast.7) | data formatting | bytes 2097152 | tf_op jit(solution)/shard_map/transpose | solution.py:539

commit v5 on v4

--- a/solution.py
+++ b/solution.py
@@ -12,12 +12,12 @@
 F32 = jnp.float32
 NX, NZ, NC, NY = 4, 8, 2, 4
 LINE = NZ * NC
-TILES = 10
+ROWS = 16 + 9 * 128
 
 
 def kernel(
-    tok_ref, emb_ref, gain_ref, w_ref, wo_ref, short_ref, skip_ref, long_ref, out_ref,
-    tprev, sf, lf, wsend, wosend, wl, e4, tt, wt, g4, oneh, band, taps, tabn, proj, pt, qt, onet, acc, stage,
+    tok_in, emb_in, gain_in, w_in, wo_in, short_in, skip_in, long_in, out_ref,
+    tok_ref, emb_ref, gain_ref, w_ref, wo_ref, short_ref, skip_ref, long_ref, in_s, tprev, sf, lf, wsend, wosend, wl, e4, tt, wt, g4, oneh, band, taps, tabn, proj, pt, qt, onet, acc, stage,
     tok_s, tok_r, fil_s, fil_r, s1_s, s1_r, s2_s, s2_r, far_r, e_s, e_r, wo_s, wo_r, t2_s, t2_r,
     ax_s, ax_r, az_s, az_r, ad_s, ad_r, wz_s, wz_r, wx_s, wx_r, wd_s, wd_r, tx_r, td_r, g_s, g_r, out_s,
 ):
@@ -57,6 +57,16 @@
 
     def gone(ref, ss):
         copy(ref, ref, ss, tok_r, mate).wait_send()
+
+    inputs = [
+        pltpu.make_async_copy(src, dst, in_s.at[n])
+        for n, (src, dst) in enumerate(
+            [
+                (w_in, w_ref), (wo_in, wo_ref), (short_in, short_ref), (skip_in, skip_ref),
+                (long_in, long_ref), (tok_in, tok_ref), (emb_in, emb_ref), (gain_in, gain_ref),
+            ]
+        )
+    ]
 
     hello = pltpu.get_barrier_semaphore()
     greeted = 0
@@ -77,6 +87,10 @@
     def _():
         pl.semaphore_signal(hello, inc=1, device_id=(turned, x), device_id_type=MESH)
 
+    for one in inputs:
+        one.start()
+    for one in inputs:
+        one.wait()
     lane32 = lax.broadcasted_iota(jnp.int32, (32, 128), 1) // 32
     for p in range(4):
         chunk = [w_ref[part, :, p * 128 : (p + 1) * 128] for part in range(3)]
@@ -125,14 +139,15 @@
 
     ids = lax.broadcasted_iota(jnp.int32, (128, 512), 1)
 
-    def onehot(tile, column):
-        oneh[tile * 128 : (tile + 1) * 128, :] = jnp.where(
-            ids == jnp.broadcast_to(column, (128, 512)), 1.0, 0.0
+    def onehot(begin, column):
+        size = column.shape[0]
+        oneh[begin : begin + size, :] = jnp.where(
+            ids[:size] == jnp.broadcast_to(column, (size, 512)), 1.0, 0.0
         ).astype(BF16)
 
     names = tok_ref[...].T
     for tile in range(8):
-        onehot(tile + 2, names[:, tile : tile + 1])
+        onehot(144 + tile * 128, names[:, tile : tile + 1])
 
     above = lax.broadcasted_iota(jnp.int32, (128, 128), 1) >= lax.broadcasted_iota(
         jnp.int32, (128, 128), 0
@@ -194,8 +209,8 @@
     ]
     got(tprev, tok_r)
     names = jnp.where(s == 0, -1, tprev[...]).T
-    for tile in range(2):
-        onehot(tile, names[:, tile + 6 : tile + 7])
+    onehot(0, names[112:128, 6:7])
+    onehot(16, names[:, 7:8])
 
     for way in range(2):
         got(wl.at[lax.rem(x + 2, NX), pl.ds(0, 8)], far_r.at[way])
@@ -341,8 +356,8 @@
             axis=1,
         )
         tabn[...] = table.T
-        for n in range(5):
-            rows = slice(n * 256, (n + 1) * 256)
+        for begin, end in ((0, 304), (304, 592), (592, 880), (880, 1168)):
+            rows = slice(begin, end)
             both = jnp.dot(oneh[rows, :], tabn[...], preferred_element_type=F32)
             for part in range(3):
                 proj[part, rows, :] = both[:, part * 128 : (part + 1) * 128]
@@ -358,17 +373,22 @@
                 total = term if total is None else total + term
             return total
 
-        def tile(n, carry):
-            row = pl.multiple_of(n * 128, 128)
-            prod, query = [], []
-            for h in range(4):
-                prod.append((fir(1, row + 32 * h, 32) * fir(2, row + 32 * h, 32)).astype(BF16))
-                query.append(fir(0, row + 32 * h, 32).astype(BF16))
-            pt[n] = jnp.concatenate(prod, axis=0).T
-            qt[n] = jnp.concatenate(query, axis=0).T
+        def tile(n, query):
+            row = pl.multiple_of(n * 128 + 16, 16)
+            pieces = [
+                (fir(1, row + 32 * h, 32) * fir(2, row + 32 * h, 32)).astype(BF16) for h in range(4)
+            ]
+            pt[n] = jnp.concatenate(pieces, axis=0).T
+            if query:
+                pieces = [fir(0, row + 32 * h, 32).astype(BF16) for h in range(4)]
+                qt[n] = jnp.concatenate(pieces, axis=0).T
+
+        def tiles(n, carry):
+            tile(n, True)
             return carry
 
-        lax.fori_loop(1, TILES, tile, 0)
+        tile(0, False)
+        lax.fori_loop(1, 9, tiles, 0)
         if late:
             late()
 
@@ -376,7 +396,7 @@
             for n in range(4):
                 g = 4 * h + n
                 ch = pl.ds(pl.multiple_of(g * 16, 16), 16)
-                prod = [pt[t, ch, :] for t in range(1, TILES)]
+                prod = [pt[t, ch, :] for t in range(9)]
                 rows = jnp.concatenate(
                     [jnp.concatenate([prod[t], prod[t + 1]], axis=1) for t in range(8)], axis=0
                 )
@@ -384,7 +404,7 @@
                 skip = jnp.broadcast_to(taps[which, p, ch, 7:8], (16, 128)).astype(BF16)
                 for t in range(8):
                     whole = conv[t * 16 : (t + 1) * 16] + skip * prod[t + 1]
-                    g4[k, p, ch, t * 128 : (t + 1) * 128] = qt[t + 2, ch, :] * whole
+                    g4[k, p, ch, t * 128 : (t + 1) * 128] = qt[t + 1, ch, :] * whole
             return carry
 
         lax.fori_loop(0, 2, groups, 0)
@@ -412,40 +432,27 @@
             cols = slice(n * 128, (n + 1) * 128)
             acc[cols, :] = jnp.dot(emb_ref[:, cols].T, onet[...], preferred_element_type=F32)
 
-    def after1():
+    def late1():
         table_own.step(3)
         table_own.across(2)
         table_far.first()
 
-    def after2():
+    def early2():
         table_own.step(4)
         table_own.across(3)
         outw.step(0)
 
-    def after3():
+    def early3():
         table_own.across(4)
-        table_far.step(1)
         outw.step(1)
 
-    def after4():
-        table_far.step(2)
-        outw.step(2)
-
-    def after5():
-        table_far.step(3)
-        outw.step(3)
-
-    def after6():
-        table_far.step(4)
-        outw.step(4)
-
-    own(1, late=after1)
+    own(1, late=late1)
     resid()
-    own(2, early=after2)
-    own(3, early=after3)
-    own(4, early=after4)
-    others(1, early=after5)
-    others(2, early=after6)
+    own(2, early=early2, late=lambda: table_far.step(1))
+    own(3, early=early3, late=lambda: table_far.step(2))
+    own(4, early=lambda: outw.step(2), late=lambda: table_far.step(3))
+    others(1, early=lambda: outw.step(3), late=lambda: table_far.step(4))
+    others(2, early=lambda: outw.step(4))
     others(3)
     others(4, early=outw.share)
     outw.shared()
@@ -498,14 +505,22 @@
     w = in_weight.transpose(1, 0, 2)
     short = short_filter.transpose(1, 0, 2)
     skip = long_skip.reshape(1, 512)
-    vmem = pl.BlockSpec(memory_space=pltpu.VMEM)
     dma = pltpu.SemaphoreType.DMA
     out = pl.pallas_call(
         kernel,
         out_shape=jax.ShapeDtypeStruct((512, 1024), BF16),
-        in_specs=[vmem] * 8,
+        in_specs=[pl.BlockSpec(memory_space=pl.ANY)] * 8,
         out_specs=pl.BlockSpec(memory_space=pl.ANY),
         scratch_shapes=[
+            pltpu.VMEM((8, 128), jnp.int32),
+            pltpu.VMEM((512, 512), BF16),
+            pltpu.VMEM((4, 1, 512), F32),
+            pltpu.VMEM((3, 32, 512), BF16),
+            pltpu.VMEM((32, 512), BF16),
+            pltpu.VMEM((3, 7, 512), F32),
+            pltpu.VMEM((1, 512), F32),
+            pltpu.VMEM((32, 128), BF16),
+            dma((8,)),
             pltpu.VMEM((8, 128), jnp.int32),
             pltpu.VMEM((2, 4, 3, 8, 128), F32),
             pltpu.VMEM((2, 32, 128), F32),
@@ -516,13 +531,13 @@
             pltpu.VMEM((2, NZ, NC, NX, 96, 128), BF16),
             pltpu.VMEM((NZ, NC, NX, 4, 32, 128), BF16),
             pltpu.VMEM((NY, 4, 128, 1024), BF16),
-            pltpu.VMEM((TILES * 128, 512), BF16),
+            pltpu.VMEM((ROWS, 512), BF16),
             pltpu.VMEM((2, 32, 256, 128), BF16),
             pltpu.VMEM((2, 4, 128, 8), F32),
             pltpu.VMEM((512, 384), BF16),
-            pltpu.VMEM((3, TILES * 128, 128), F32),
-            pltpu.VMEM((TILES, 128, 128), BF16),
-            pltpu.VMEM((TILES, 128, 128), BF16),
+            pltpu.VMEM((3, ROWS, 128), F32),
+            pltpu.VMEM((9, 128, 128), BF16),
+            pltpu.VMEM((9, 128, 128), BF16),
             pltpu.VMEM((512, 1024), BF16),
             pltpu.VMEM((512, 1024), F32),
             pltpu.VMEM((512, 1024), BF16),

time: 71.2 us -> 69.2 us (0.972)
  Pallas kernels: 68.8 us -> 66.8 us
    pallas_call x1, Pallas kernels: 68.8 us -> 66.8 us  [body(): pl.pallas_call(kernel, out_shape=jax.ShapeDtypeStruct((512, 1024), BF16),...]
where the time goes in v5:
time: 69.2 us; the launch traced here: 69 us
  Pallas kernels  66.8 us (97%)
  local copies, waits for them, and re-layouts  2.28 us (3%)
    pallas_call x1, Pallas kernels, body(): pl.pallas_call(kernel, out_shape=jax.ShapeDtypeStruct((512, 1024), BF16),...  66.8 us
    transpose x1, local copies, waits for them, and re-layouts, body(): return out.T  2.28 us

profile of v5, /device:TPU:1, one launch (start us, length us, event | category | flops | bytes accessed | tf_op | source)
XLA Modules:
  0.0 69.0 jit_solution(13320523847135764876)
XLA Ops:
  0.0 66.8 %shard_map.82 = bf16[512,1024]{1,0:T(8,128)(2,1)} custom-call(s32[8,128]{1,0:T(8,128)} %bitcast.12, bf16[512,512]{1,0:T(8,128)(2,1)} %emb_in.1, f32[4,1,512]{2,1,0:T(1,128)} %bitcast.11, bf16[3,32,512]{2,1,0:T(8,128)(2,1)} %bitcast.8, bf16[32,512]{1,0:T(8,128)(2,1)} %bitcast.10, f32[3,7,512]{2,1,0:T(8,128)} %bitcast.9, f32[1,512]{1,0:T(1,128)} %bitcast.13, ...), custom_call_target="tpu_custom_call" | custom-call | tf_op jit(solution)/shard_map/pallas_call | solution.py:509
  66.8 2.3 %copy.9 = bf16[1024,512]{1,0:T(8,128)(2,1)} copy(bf16[1024,512]{0,1:T(8,128)(2,1)} %bitcast.7) | data formatting | bytes 2097152 | tf_op jit(solution)/shard_map/transpose | solution.py:554

commit v6 on v5

--- a/solution.py
+++ b/solution.py
@@ -446,11 +446,14 @@
         table_own.across(4)
         outw.step(1)
 
+    def late4():
+        resid()
+        table_far.step(3)
+
     own(1, late=late1)
-    resid()
     own(2, early=early2, late=lambda: table_far.step(1))
     own(3, early=early3, late=lambda: table_far.step(2))
-    own(4, early=lambda: outw.step(2), late=lambda: table_far.step(3))
+    own(4, early=lambda: outw.step(2), late=late4)
     others(1, early=lambda: outw.step(3), late=lambda: table_far.step(4))
     others(2, early=lambda: outw.step(4))
     others(3)

time: 69.2 us -> 69.4 us (level)
  no operation moved by 1% of the time
where the time goes in v6:
time: 69.4 us; the launch traced here: 69.3 us
  Pallas kernels  67 us (97%)
  local copies, waits for them, and re-layouts  2.28 us (3%)
    pallas_call x1, Pallas kernels, body(): pl.pallas_call(kernel, out_shape=jax.ShapeDtypeStruct((512, 1024), BF16),...  67 us
    transpose x1, local copies, waits for them, and re-layouts, body(): return out.T  2.28 us

profile of v6, /device:TPU:1, one launch (start us, length us, event | category | flops | bytes accessed | tf_op | source)
XLA Modules:
  0.0 69.3 jit_solution(10399562031734737531)
XLA Ops:
  0.0 67.0 %shard_map.82 = bf16[512,1024]{1,0:T(8,128)(2,1)} custom-call(s32[8,128]{1,0:T(8,128)} %bitcast.12, bf16[512,512]{1,0:T(8,128)(2,1)} %emb_in.1, f32[4,1,512]{2,1,0:T(1,128)} %bitcast.11, bf16[3,32,512]{2,1,0:T(8,128)(2,1)} %bitcast.8, bf16[32,512]{1,0:T(8,128)(2,1)} %bitcast.10, f32[3,7,512]{2,1,0:T(8,128)} %bitcast.9, f32[1,512]{1,0:T(1,128)} %bitcast.13, ...), custom_call_target="tpu_custom_call" | custom-call | tf_op jit(solution)/shard_map/pallas_call | solution.py:512
  67.0 2.3 %copy.9 = bf16[1024,512]{1,0:T(8,128)(2,1)} copy(bf16[1024,512]{0,1:T(8,128)(2,1)} %bitcast.7) | data formatting | bytes 2097152 | tf_op jit(solution)/shard_map/transpose | solution.py:557
